TPU v7x, 512 devices: a whole 4x8x8 slice. The times are simulated.
512 devices in a mesh: cam: 128 (over y, z, core), proj: 4 (over x).
Axes of the slice: x: 4, y: 8, z: 8, core: 2. Of those that a mesh axis runs over, the one named last changes fastest.
Arguments:
- transport: bfloat16 [65536, 16384], P('cam', 'proj'), may hold values from -0.09375 to 0.09375
- test_panel: bfloat16 [16384, 32], P(('proj', 'cam')), may hold values from -6 to 6
Outputs:
- basis: float32 [65536, 32], P('cam')
- coimage: float32 [16384, 32], P(('proj', 'cam'))
All inputs are finite; a program needn't handle non-finite values.
Results may differ from a plain program's by a relative error of at most 0.0027.
Values may be sent and summed in bfloat16 or wider, within the bound.
No kernel may reach another device: no remote copies, remote signals or barrier semaphores. Data moves between devices by JAX's collectives and lax.ppermute only.
A program may use at most 64 MiB of HBM per device.

v0:
```python
import jax
import jax.numpy as jnp
from jax import lax
from jax.sharding import PartitionSpec as P

ITERS = 2


def small_gram(block):
    return jnp.dot(
        block.T, block, precision=lax.Precision.HIGHEST, preferred_element_type=jnp.float32
    )


def apply_factor(gram, block):
    lower = jnp.linalg.cholesky(gram)
    return jax.scipy.linalg.solve_triangular(lower, block.T, lower=True).T


def on_device(transport, test_panel):
    rows_here = transport.shape[0]
    total_rows = rows_here * lax.axis_size("cam")
    panel_piece = test_panel
    basis = None
    coimage = None
    for step in range(ITERS):
        partial_sketch = jnp.dot(
            transport,
            lax.all_gather(panel_piece, "cam", axis=0, tiled=True),
            preferred_element_type=jnp.float32,
        )
        sketch = lax.psum(partial_sketch, "proj")
        gram = lax.psum(small_gram(sketch), "cam") / total_rows
        basis = apply_factor(gram, sketch)
        basis_low = basis.astype(jnp.bfloat16)
        last = step + 1 == ITERS
        coimage = lax.psum_scatter(
            lax.dot_general(
                transport, basis_low, (((0,), (0,)), ((), ())), preferred_element_type=jnp.float32
            ),
            "cam",
            scatter_dimension=0,
            tiled=True,
        )
        if not last:
            panel_piece = coimage.astype(jnp.bfloat16)
    return (basis, coimage)


def solution(mesh):
    placed = (P("cam", "proj"), P(("proj", "cam"), None))
    return jax.shard_map(
        on_device,
        mesh=mesh,
        in_specs=placed,
        out_specs=(P("cam", None), P(("proj", "cam"), None)),
        check_vma=False,
    )
```

profile of v0, /device:TPU:6, one launch (start us, length us, event | category | flops | bytes accessed | tf_op | source)
XLA Modules:
  0.0 1628.0 jit_solution(12464336792124813939)
XLA Ops:
  7.2 57.9 %all_gather.6 = bf16[4096,32]{1,0:T(8,128)(2,1)S(1)} all-gather(bf16[32,32]{1,0:T(8,128)(2,1)} %param.6), channel_id=1, replica_groups=mesh['cam'=128,'proj'=4] {'cam'}, dimensions={0}, use_global_device_ids=true | all-gather | bytes 264192 | tf_op jit(solution)/shard_map/all_gather | solution.py:29
  65.1 4.2 fusion.11
  69.3 0.0 reduce-scatter.7.cloned.1.call-start
  69.3 46.0 %all-reduce.3.cloned.1.call-done = f32[512,32]{0,1:T(8,128)} async-done(((f32[512,32]{0,1:T(8,128)}), f32[512,32]{0,1:T(8,128)}) %all-reduce.3.cloned.1.call-update) | async-done | bytes 65552 | tf_op jit(solution)/shard_map/psum | solution.py:32
  115.3 1.1 fusion.12
  116.4 494.6 %psum.29 = f32[32,32]{0,1:T(8,128)S(1)} all-reduce(f32[32,32]{0,1:T(8,128)S(1)} %fusion.12), channel_id=1, replica_groups=mesh['cam'=128,'proj'=4] {'cam'}, use_global_device_ids=true, to_apply=%region_1.0 | all-reduce | flops 1024 | bytes 8192 | tf_op jit(solution)/shard_map/psum | solution.py:33
  611.0 0.1 copy.10
  611.1 2.9 cholesky.44
  614.0 0.6 compare_reduce_fusion.1
  614.7 0.7 fusion.3
  615.3 2.4 custom-call.6
  617.8 1.1 convolution_convert_fusion
  618.9 3.0 convolution_bitcast_fusion.1
  621.9 2.0 copy.17
  623.9 0.0 all-reduce.5.cloned.1.call-start
  624.0 193.2 %reduce-scatter.7.cloned.1.call-done = f32[32,32]{1,0:T(8,128)} async-done(((f32[4096,32]{1,0:T(8,128)}), f32[32,32]{1,0:T(8,128)}) %reduce-scatter.7.cloned.1.call-update) | async-done | bytes 4112
  817.2 0.8 copy.18
  818.0 0.1 copy.11
  818.1 49.0 %all_gather.7 = bf16[4096,32]{1,0:T(8,128)(2,1)S(1)} all-gather(bf16[32,32]{1,0:T(8,128)(2,1)S(1)} %copy.11), channel_id=1, replica_groups=mesh['cam'=128,'proj'=4] {'cam'}, dimensions={0}, use_global_device_ids=true | all-gather | bytes 264192 | tf_op jit(solution)/shard_map/all_gather | solution.py:29
  867.0 4.2 convolution_bitcast_fusion.3
  871.3 48.3 %all-reduce.5.cloned.1.call-done = f32[512,32]{0,1:T(8,128)} async-done(((f32[512,32]{0,1:T(8,128)}), f32[512,32]{0,1:T(8,128)}) %all-reduce.5.cloned.1.call-update) | async-done | bytes 65552 | tf_op jit(solution)/shard_map/psum | solution.py:32
  919.6 1.1 fusion.13
  920.8 494.6 %psum.31 = f32[32,32]{0,1:T(8,128)S(1)} all-reduce(f32[32,32]{0,1:T(8,128)S(1)} %fusion.13), channel_id=1, replica_groups=mesh['cam'=128,'proj'=4] {'cam'}, use_global_device_ids=true, to_apply=%region_6.9 | all-reduce | flops 1024 | bytes 8192 | tf_op jit(solution)/shard_map/psum | solution.py:33
  1415.3 0.1 copy.13
  1415.4 2.9 cholesky.55
  1418.4 0.6 compare_reduce_fusion
  1419.0 0.7 fusion.4
  1419.7 2.4 custom-call.7
  1422.1 1.1 convolution_bitcast_fusion.2
  1423.3 3.0 convolution_bitcast_fusion
  1426.3 2.0 copy.19
  1428.3 193.2 %reduce-scatter.9.cloned.1.call-done = f32[32,32]{1,0:T(8,128)} async-done(((f32[4096,32]{1,0:T(8,128)}), f32[32,32]{1,0:T(8,128)}) %reduce-scatter.9.cloned.1.call-update) | async-done | bytes 4112
  (14 shorter events, 0.2 us)
Async XLA Ops:
  7.2 108.1 %all-reduce.3.cloned.1.call-start = ((), (), s32[]{:S(2)}) async-start(), calls=%async_computation.2 | async-start | bytes 131072 | tf_op jit(solution)/shard_map/psum | solution.py:32
  69.3 747.9 %reduce-scatter.7.cloned.1.call-start = ((), (), s32[]{:S(2)}) async-start(), calls=%async_computation.4 | async-start | bytes 2113536
  623.9 295.7 %all-reduce.5.cloned.1.call-start = ((), (), s32[]{:S(2)}) async-start(), calls=%async_computation.3 | async-start | bytes 131072 | tf_op jit(solution)/shard_map/psum | solution.py:32
  871.3 750.2 %reduce-scatter.9.cloned.1.call-start = ((), (), s32[]{:S(2)}) async-start(), calls=%async_computation.5 | async-start | bytes 2113536
  1423.2 5.0 copy-start
Sparse Core Ops, SparseCore 0:
  69.4 45.8 all-reduce.2
  624.0 193.1 reduce-scatter.6
  871.4 48.1 all-reduce.4
  1428.4 192.9 reduce-scatter.8
where the time goes:
time: 1630 us
  blocking collectives  1100 us (67%)
  waiting for transfers between devices  481 us (30%)
  matrix products  18.9 us (1%)
    psum x2, blocking collectives, on_device(): gram = lax.psum(small_gram(sketch), 'cam') / total_rows  989 us
    unnamed x6, waiting for transfers between devices  386 us
    all_gather x2, blocking collectives, on_device(): lax.all_gather(panel_piece, 'cam', axis=0, tiled=True)  107 us
    psum x2, waiting for transfers between devices, on_device(): sketch = lax.psum(partial_sketch, 'proj')  94.3 us
  transfers between devices with their start and end apart: 4, of which 4 were waited for; matrix products, arithmetic and copies ran while one was open for 0% of the time, Pallas kernels for 0%

commit v1 on v0

v1 whole, which is shorter than its diff:
```python
import jax
import jax.numpy as jnp
import numpy as np
from jax import lax
from jax.sharding import Mesh
from jax.sharding import PartitionSpec as P

ITERS = 2
CHIPS = ("y", "z")
HIGHEST = lax.Precision.HIGHEST


def pack(square):
    return square.reshape(4, 8, 32).transpose(1, 0, 2).reshape(8, 128)


def unpack(tile):
    return tile.reshape(8, 4, 32).transpose(1, 0, 2).reshape(32, 32)


def gather(tile):
    other = lax.ppermute(tile, "core", [(0, 1), (1, 0)])
    first = lax.axis_index("core") == 0
    pair = jnp.concatenate([jnp.where(first, tile, other), jnp.where(first, other, tile)])
    chips = lax.axis_size(CHIPS)
    copies = jnp.broadcast_to(pair, (chips,) + pair.shape)
    return lax.all_to_all(copies, CHIPS, 0, 0).reshape(2 * chips, 8, 128)


def sum_over_x(block):
    copies = jnp.broadcast_to(block, (lax.axis_size("x"),) + block.shape)
    return jnp.sum(lax.all_to_all(copies, "x", 0, 0), axis=0)


def reduce_tiles(tiles, gram):
    chips = lax.axis_size(CHIPS)
    halves = tiles.reshape(chips, 2, 8, 128).transpose(1, 0, 2, 3)
    grams = jnp.broadcast_to(gram, (2, 1, 8, 128))
    half = jnp.sum(lax.all_to_all(jnp.concatenate([halves, grams], axis=1), "core", 0, 0), axis=0)
    message = jnp.concatenate(
        [half[:chips], jnp.broadcast_to(half[chips:], (chips, 8, 128))], axis=1
    )
    total = jnp.sum(lax.all_to_all(message, CHIPS, 0, 0), axis=0)
    return total[:8], total[8:]


def inverse_factor(gram):
    lower = jnp.linalg.cholesky(gram)
    eye = jnp.eye(gram.shape[0], dtype=gram.dtype)
    return jax.scipy.linalg.solve_triangular(lower, eye, lower=True).T


def on_device(transport, test_panel):
    total_rows = transport.shape[0] * lax.axis_size(("y", "z", "core"))
    tile = pack(test_panel)
    basis = None
    for step in range(ITERS):
        tiles = gather(tile)
        panel = tiles.reshape(-1, 8, 4, 32).transpose(0, 2, 1, 3).reshape(-1, 32)
        partial = jnp.dot(transport, panel, preferred_element_type=jnp.float32)
        packed = partial.reshape(4, 128, 32).transpose(1, 0, 2).reshape(128, 128)
        sketch = sum_over_x(packed).reshape(128, 4, 32).transpose(1, 0, 2).reshape(512, 32)
        gram = jnp.dot(sketch.T, sketch, precision=HIGHEST, preferred_element_type=jnp.float32)
        high = sketch.astype(jnp.bfloat16)
        low = (sketch - high.astype(jnp.float32)).astype(jnp.bfloat16)
        both = lax.dot_general(
            transport,
            jnp.concatenate([high, low], axis=1),
            (((0,), (0,)), ((), ())),
            preferred_element_type=jnp.float32,
        )
        product = both[:, :32] + both[:, 32:]
        pieces = product.reshape(-1, 4, 8, 32).transpose(0, 2, 1, 3).reshape(-1, 8, 128)
        piece, gram = reduce_tiles(pieces, pack(gram))
        inverse = inverse_factor(unpack(gram) / total_rows)
        coimage = jnp.dot(unpack(piece), inverse, precision=HIGHEST)
        if step + 1 < ITERS:
            tile = pack(coimage.astype(jnp.bfloat16))
        else:
            basis = jnp.dot(sketch, inverse, precision=HIGHEST)
    return (basis, coimage)


def solution(mesh):
    sizes = {"cam": (("y", 8), ("z", 8), ("core", 2)), "proj": (("x", 4),)}
    names = [name for axis in mesh.axis_names for name, _ in sizes[axis]]
    shape = [size for axis in mesh.axis_names for _, size in sizes[axis]]
    fine = Mesh(np.asarray(mesh.devices).reshape(shape), names)
    rows = ("y", "z", "core")
    return jax.shard_map(
        on_device,
        mesh=fine,
        in_specs=(P(rows, "x"), P(("x",) + rows, None)),
        out_specs=(P(rows, None), P(("x",) + rows, None)),
        check_vma=False,
    )
```

time: 1630 us -> 179 us (0.11)
  blocking collectives: 1100 us -> 126 us
  waiting for transfers between devices: 481 us -> 2.24 us
    psum x2 -> x0, blocking collectives: 989 us -> none  [on_device(): gram = lax.psum(small_gram(sketch), 'cam') / total_rows]
    unnamed x6 -> x0, waiting for transfers between devices: 386 us -> none
    all_to_all x0 -> x8, blocking collectives: none -> 126 us  [the longest x2 52.6 us: gather(): return lax.all_to_all(copies, CHIPS, 0, 0).reshape(2 * chips, 8, 128)]
    all_gather x2 -> x0, blocking collectives: 107 us -> none  [on_device(): lax.all_gather(panel_piece, 'cam', axis=0, tiled=True)]
    psum x2 -> x0, waiting for transfers between devices: 94.3 us -> none  [on_device(): sketch = lax.psum(partial_sketch, 'proj')]
  transfers between devices with their start and end apart: 4 -> 2, of which waited for: 4 -> 2; matrix products, arithmetic and copies ran while one was open for 0% -> 0% of each run, Pallas kernels for 0% -> 0%
where the time goes in v1:
time: 179 us; the launch traced here: 176 us
  blocking collectives  126 us (70%)
  matrix products  15.9 us (9%)
  other arithmetic  13.9 us (8%)
  local copies, waits for them, and re-layouts  13.4 us (7%)
  starting transfers between devices  3.82 us (2%)
  waiting for transfers between devices  2.24 us (1%)
    all_to_all x2, blocking collectives, gather(): return lax.all_to_all(copies, CHIPS, 0, 0).reshape(2 * chips, 8, 128)  52.6 us
    all_to_all x2, blocking collectives, reduce_tiles(): total = jnp.sum(lax.all_to_all(message, CHIPS, 0, 0), axis=0)  46.4 us
    all_to_all x2, blocking collectives, sum_over_x(): return jnp.sum(lax.all_to_all(copies, 'x', 0, 0), axis=0)  18.2 us
    all_to_all x2, blocking collectives, reduce_tiles(): lax.all_to_all(jnp.concatenate([halves, grams], axis=1), 'core', 0, 0)  8.26 us
    another operation x6, other arithmetic, inverse_factor(): lower = jnp.linalg.cholesky(gram)  7.19 us
    dot_general x2, matrix products, on_device(): partial = jnp.dot(transport, panel, preferred_element_type=jnp.float32)  7.14 us
    another operation x4, other arithmetic, inverse_factor(): return jax.scipy.linalg.solve_triangular(lower, eye, lower=True).T  6.17 us
    dot_general x2, matrix products, on_device(): lax.dot_general(transport, jnp.concatenate([high, low], axis=1), (((0,),...  6.13 us
  transfers between devices with their start and end apart: 2, of which 2 were waited for; matrix products, arithmetic and copies ran while one was open for 0% of the time, Pallas kernels for 0%

profile of v1, /device:TPU:6, one launch (start us, length us, event | category | flops | bytes accessed | tf_op | source)
XLA Modules:
  0.0 175.9 jit_solution(1592446106458124741)
XLA Ops:
  0.6 0.7 copy.145
  1.4 1.9 %collective-permute-start = (bf16[8,128]{1,0:T(8,128)(2,1)S(1)}, bf16[8,128]{1,0:T(8,128)(2,1)S(1)}, u32[]{:S(2)}, u32[]{:S(2)}) collective-permute-start(bf16[8,128]{1,0:T(8,128)(2,1)S(1)} %reshape.95), channel_id=1, source_target_pairs={{0,4},{4,0},{1,5},{5,1},{2,6},{6,2},{3,7},{7,3},{8,12},{12,8},{9,1... | collective-permute-start | bytes 6152 | tf_op jit(solution)/shard_map/ppermute | solution.py:22
  3.3 1.1 collective-permute-done
  4.5 31.7 %all_to_all.40 = bf16[64,16,128]{2,1,0:T(8,128)(2,1)S(1)} all-to-all(bf16[64,16,128]{2,1,0:T(8,128)(2,1)S(1)} %broadcast_in_dim.33), channel_id=1, replica_groups=mesh['y'=8,'z'=8,'core'=2,'x'=4] {'y','z'}, dimensions={0} | all-to-all | bytes 524288 | tf_op jit(solution)/shard_map/all_to_all | solution.py:27
  36.8 3.6 %convolution_bitcast_fusion.3 = f32[4,4,8,128]{3,2,1,0:T(8,128)S(1)} fusion(bf16[4096,32]{1,0:T(8,128)(2,1)S(1)} %bitcast.148, bf16[512,4096]{1,0:T(8,128)(2,1)} %param.5), kind=kOutput, calls=%fused_computation.3 | convolution fusion | flops 134217728 | bytes 4521984 | tf_op jit(solution)/shard_map/dot_general | solution.py:60
  40.5 9.2 %all_to_all.41 = f32[4,128,128]{2,1,0:T(8,128)S(1)} all-to-all(f32[4,128,128]{2,1,0:T(8,128)S(1)} %broadcast_in_dim.34), channel_id=1, replica_groups=mesh['y'=8,'z'=8,'core'=2,'x'=4] {'x'}, dimensions={0} | all-to-all | bytes 524288 | tf_op jit(solution)/shard_map/all_to_all | solution.py:32
  49.9 3.1 %convolution_bitcast_fusion.1 = f32[4096,64]{0,1:T(8,128)S(1)} fusion(bf16[512,4096]{1,0:T(8,128)(2,1)} %param.5, bf16[512,32]{0,1:T(8,128)(2,1)S(1)} %fusion.4, bf16[512,32]{0,1:T(8,128)(2,1)S(1)} %bitcast.167), kind=kOutput, calls=%fused_computation.1 | convolution fusion | flops 268566528 | bytes 5308416 | tf_op jit(solution)/shard_map/dot_general | solution.py:66
  53.0 0.6 copy.76
  53.6 1.9 %copy.77 = f32[128,8,4,32]{3,2,1,0:T(4,128)} copy(f32[128,8,4,32]{3,1,2,0:T(8,128)S(1)} %bitcast.144) | data formatting | bytes 1048576 | tf_op jit(solution)/shard_map/transpose | solution.py:73
  55.5 2.4 %reshape_reshape.13 = f32[64,2,8,128]{3,2,1,0:T(8,128)S(1)} reshape(f32[128,8,4,32]{3,2,1,0:T(4,128)} %copy.77) | data formatting | bytes 1048576 | tf_op jit(solution)/shard_map/reshape;reshape | solution.py:37
  58.4 4.1 %all_to_all.42 = f32[2,65,8,128]{3,2,1,0:T(8,128)S(1)} all-to-all(f32[2,65,8,128]{3,2,1,0:T(8,128)S(1)} %copy.79), channel_id=1, replica_groups=mesh['y'=8,'z'=8,'core'=2,'x'=4] {'core'}, dimensions={0} | all-to-all | bytes 1064960 | tf_op jit(solution)/shard_map/all_to_all | solution.py:39
  62.7 23.2 %all_to_all.43 = f32[64,16,128]{2,1,0:T(8,128)S(1)} all-to-all(f32[64,16,128]{2,1,0:T(8,128)S(1)} %pad_maximum_fusion.2), channel_id=1, replica_groups=mesh['y'=8,'z'=8,'core'=2,'x'=4] {'y','z'}, dimensions={0} | all-to-all | bytes 1048576 | tf_op jit(solution)/shard_map/all_to_all | solution.py:43
  86.1 2.9 %cholesky.44 = f32[32,32]{1,0:T(8,128)S(1)} custom-call(f32[32,32]{1,0:T(8,128)S(1)} %fusion.25), custom_call_target="Cholesky" | custom-call | tf_op jit(solution)/shard_map/jit(cholesky)/cholesky | solution.py:48
  89.1 0.6 compare_reduce_fusion.1
  89.7 0.7 fusion.18
  90.4 2.4 %custom-call.6 = f32[1,32,32]{1,2,0:T(8,128)S(1)} custom-call(f32[1,32,32]{2,1,0:T(8,128)S(1)} %fusion.18), custom_call_target="InvertDiagBlocksLowerTriangular" | custom-call | tf_op jit(solution)/shard_map/jit(_solve_triangular)/triangular_solve | solution.py:50
  93.4 1.9 %collective-permute-start.1 = (bf16[8,128]{1,0:T(8,128)(2,1)S(1)}, bf16[8,128]{1,0:T(8,128)(2,1)S(1)}, u32[]{:S(2)}, u32[]{:S(2)}) collective-permute-start(bf16[8,128]{1,0:T(8,128)(2,1)S(1)} %reshape.106), channel_id=1, source_target_pairs={{0,4},{4,0},{1,5},{5,1},{2,6},{6,2},{3,7},{7,3},{8,12},{12,8},{9,1... | collective-permute-start | bytes 6152 | tf_op jit(solution)/shard_map/ppermute | solution.py:22
  95.3 1.1 collective-permute-done.1
  96.5 21.0 %all_to_all.44 = bf16[64,16,128]{2,1,0:T(8,128)(2,1)S(1)} all-to-all(bf16[64,16,128]{2,1,0:T(8,128)(2,1)S(1)} %broadcast_in_dim.38), channel_id=1, replica_groups=mesh['y'=8,'z'=8,'core'=2,'x'=4] {'y','z'}, dimensions={0} | all-to-all | bytes 524288 | tf_op jit(solution)/shard_map/all_to_all | solution.py:27
  118.1 3.6 %convolution_bitcast_fusion.2 = f32[4,4,8,128]{3,2,1,0:T(8,128)S(1)} fusion(bf16[4096,32]{1,0:T(8,128)(2,1)S(1)} %bitcast.149, bf16[512,4096]{1,0:T(8,128)(2,1)} %param.5), kind=kOutput, calls=%fused_computation.2 | convolution fusion | flops 134217728 | bytes 4521984 | tf_op jit(solution)/shard_map/dot_general | solution.py:60
  121.8 9.1 %all_to_all.45 = f32[4,128,128]{2,1,0:T(8,128)S(1)} all-to-all(f32[4,128,128]{2,1,0:T(8,128)S(1)} %broadcast_in_dim.39), channel_id=1, replica_groups=mesh['y'=8,'z'=8,'core'=2,'x'=4] {'x'}, dimensions={0} | all-to-all | bytes 524288 | tf_op jit(solution)/shard_map/all_to_all | solution.py:32
  131.0 3.1 %convolution_bitcast_fusion = f32[4096,64]{0,1:T(8,128)S(1)} fusion(bf16[512,4096]{1,0:T(8,128)(2,1)} %param.5, bf16[512,32]{0,1:T(8,128)(2,1)S(1)} %fusion.3, bf16[512,32]{0,1:T(8,128)(2,1)S(1)} %bitcast.168), kind=kOutput, calls=%fused_computation | convolution fusion | flops 268566528 | bytes 5308416 | tf_op jit(solution)/shard_map/dot_general | solution.py:66
  134.7 1.9 %copy.90 = f32[128,8,4,32]{3,2,1,0:T(4,128)} copy(f32[128,8,4,32]{3,1,2,0:T(8,128)S(1)} %bitcast.145) | data formatting | bytes 1048576 | tf_op jit(solution)/shard_map/transpose | solution.py:73
  136.6 2.4 %reshape_reshape.15 = f32[64,2,8,128]{3,2,1,0:T(8,128)S(1)} reshape(f32[128,8,4,32]{3,2,1,0:T(4,128)} %copy.90) | data formatting | bytes 1048576 | tf_op jit(solution)/shard_map/reshape;reshape | solution.py:37
  139.5 4.1 %all_to_all.46 = f32[2,65,8,128]{3,2,1,0:T(8,128)S(1)} all-to-all(f32[2,65,8,128]{3,2,1,0:T(8,128)S(1)} %copy.92), channel_id=1, replica_groups=mesh['y'=8,'z'=8,'core'=2,'x'=4] {'core'}, dimensions={0} | all-to-all | bytes 1064960 | tf_op jit(solution)/shard_map/all_to_all | solution.py:39
  143.8 23.2 %all_to_all.47 = f32[64,16,128]{2,1,0:T(8,128)S(1)} all-to-all(f32[64,16,128]{2,1,0:T(8,128)S(1)} %pad_maximum_fusion.3), channel_id=1, replica_groups=mesh['y'=8,'z'=8,'core'=2,'x'=4] {'y','z'}, dimensions={0} | all-to-all | bytes 1048576 | tf_op jit(solution)/shard_map/all_to_all | solution.py:43
  167.3 2.9 %cholesky.55 = f32[32,32]{1,0:T(8,128)S(1)} custom-call(f32[32,32]{1,0:T(8,128)S(1)} %fusion.23), custom_call_target="Cholesky" | custom-call | tf_op jit(solution)/shard_map/jit(cholesky)/cholesky | solution.py:48
  170.2 0.6 compare_reduce_fusion
  170.9 0.7 fusion.19
  171.5 2.4 %custom-call.7 = f32[1,32,32]{1,2,0:T(8,128)S(1)} custom-call(f32[1,32,32]{2,1,0:T(8,128)S(1)} %fusion.19), custom_call_target="InvertDiagBlocksLowerTriangular" | custom-call | tf_op jit(solution)/shard_map/jit(_solve_triangular)/triangular_solve | solution.py:50
  174.3 0.8 fusion.1
  175.1 0.8 fusion.20
  (75 shorter events, 5.1 us)
Async XLA Ops:
  1.4 3.0 %collective-permute-start = (bf16[8,128]{1,0:T(8,128)(2,1)S(1)}, bf16[8,128]{1,0:T(8,128)(2,1)S(1)}, u32[]{:S(2)}, u32[]{:S(2)}) collective-permute-start(bf16[8,128]{1,0:T(8,128)(2,1)S(1)} %reshape.95), channel_id=1, source_target_pairs={{0,4},{4,0},{1,5},{5,1},{2,6},{6,2},{3,7},{7,3},{8,12},{12,8},{9,1... | collective-permute-start | bytes 6152 | tf_op jit(solution)/shard_map/ppermute | solution.py:22
  93.4 3.0 %collective-permute-start.1 = (bf16[8,128]{1,0:T(8,128)(2,1)S(1)}, bf16[8,128]{1,0:T(8,128)(2,1)S(1)}, u32[]{:S(2)}, u32[]{:S(2)}) collective-permute-start(bf16[8,128]{1,0:T(8,128)(2,1)S(1)} %reshape.106), channel_id=1, source_target_pairs={{0,4},{4,0},{1,5},{5,1},{2,6},{6,2},{3,7},{7,3},{8,12},{12,8},{9,1... | collective-permute-start | bytes 6152 | tf_op jit(solution)/shard_map/ppermute | solution.py:22

commit v2 on v0

v2 whole, which is shorter than its diff:
```python
import functools

import jax
import jax.numpy as jnp
import numpy as np
from jax import lax
from jax.experimental import pallas as pl
from jax.experimental.pallas import tpu as pltpu
from jax.sharding import Mesh
from jax.sharding import PartitionSpec as P

CHIPS = ("y", "z")
RANK = 32
HIGHEST = lax.Precision.HIGHEST
F32 = jnp.float32
BF16 = jnp.bfloat16
VMEM = pl.BlockSpec(memory_space=pltpu.VMEM)
NT = (((1,), (1,)), ((), ()))
TN = (((0,), (0,)), ((), ()))


def kernel_call(body, outs, flops, moved, *args):
    return pl.pallas_call(
        body,
        out_shape=outs,
        in_specs=[VMEM] * len(args),
        out_specs=jax.tree.map(lambda _: VMEM, outs),
        compiler_params=pltpu.CompilerParams(vmem_limit_bytes=24 << 20),
        cost_estimate=pl.CostEstimate(flops=flops, bytes_accessed=moved, transcendentals=0),
    )(*args)


def lanes_of(shape):
    return lax.broadcasted_iota(jnp.int32, shape, len(shape) - 1)


def pack_square(square):
    lane = lanes_of((8, 128))
    out = jnp.where(lane < 32, square[0:8], 0.0)
    for q in range(1, 4):
        block = pltpu.roll(square[8 * q : 8 * q + 8], 32 * q, axis=1)
        out = jnp.where((lane >= 32 * q) & (lane < 32 * q + 32), block, out)
    return out


def unpack_square(tile):
    return jnp.concatenate([tile] + [pltpu.roll(tile, 128 - 32 * q, axis=1) for q in range(1, 4)])


def inverse_factor(gram):
    lane = lanes_of((RANK, 128))
    row = lax.broadcasted_iota(jnp.int32, (RANK, 128), 0)
    work = jnp.where(lane < RANK, gram, jnp.where(lane == row + RANK, 1.0, 0.0))
    pivots = jnp.ones((RANK, 128), F32)
    width = 8
    for start in range(0, RANK, width):
        columns = [
            jnp.broadcast_to(work[:, start + i : start + i + 1], (RANK, 128)) for i in range(width)
        ]
        for i in range(width):
            k = start + i
            pivot = jnp.broadcast_to(columns[i][k : k + 1], (RANK, 128))
            pivots = jnp.where(row == k, pivot, pivots)
            factor = jnp.where(row > k, columns[i] / pivot, 0.0)
            for later in range(i + 1, width):
                columns[later] = columns[later] - factor * columns[later][k : k + 1]
            work = work - factor * work[k : k + 1]
    return (work / jnp.sqrt(pivots))[:, RANK : 2 * RANK]


def first_sketch(tiles_ref, transport_ref, out_ref):
    chips, cols = tiles_ref.shape[0], transport_ref.shape[1]
    lane = lanes_of((16, 128))
    masks = [(lane >= 32 * q) & (lane < 32 * q + 32) for q in range(4)]
    total = jnp.zeros((transport_ref.shape[0], 128), F32)
    group = 8
    for start in range(0, chips, group):
        rows = []
        for chip in range(start, start + group):
            tile = tiles_ref[chip]
            rows += [jnp.where(mask, tile, jnp.zeros_like(tile)) for mask in masks]
        at = start * (cols // chips)
        total += jnp.dot(
            transport_ref[:, at : at + group * (cols // chips)],
            jnp.concatenate(rows),
            preferred_element_type=F32,
        )
    turned = total.T
    sketch = (turned[0:32] + turned[32:64]) + (turned[64:96] + turned[96:128])
    for copy in range(out_ref.shape[0]):
        out_ref[copy] = sketch


def next_sketch(panel_ref, transport_ref, out_ref):
    groups, _, width = panel_ref.shape
    sketch = jnp.zeros((RANK, transport_ref.shape[0]), F32)
    for g in range(groups):
        sketch += lax.dot_general(
            panel_ref[g],
            transport_ref[:, g * width : (g + 1) * width],
            NT,
            preferred_element_type=F32,
        )
    for copy in range(out_ref.shape[0]):
        out_ref[copy] = sketch


def product(parts_ref, transport_ref):
    sketch = (parts_ref[0] + parts_ref[1]) + (parts_ref[2] + parts_ref[3])
    gram = lax.dot_general(sketch, sketch, NT, precision=HIGHEST, preferred_element_type=F32)
    gram = jnp.concatenate([gram, jnp.zeros((RANK, 128 - RANK), F32)], axis=1)
    high = sketch.astype(BF16)
    low = (sketch - high.astype(F32)).astype(BF16)
    both = jnp.concatenate([high, low])

    def columns(at, width):
        out = jnp.dot(both, transport_ref[:, at : at + width], preferred_element_type=F32)
        return out[:RANK] + out[RANK:]

    return sketch, pack_square(gram), columns


def middle_product(parts_ref, transport_ref, out_ref):
    cores, groups, height, _ = out_ref.shape
    tiles = height // 8 - 1
    width = tiles // 4 * 128
    _, gram, columns = product(parts_ref, transport_ref)
    for core in range(cores):
        for g in range(groups):
            block = columns((core * groups + g) * width, width)
            for t in range(tiles):
                a, c = t % 4, t // 4
                out_ref[core, g, 8 * t : 8 * t + 8] = block[8 * a : 8 * a + 8, 128 * c : 128 * c + 128]
            out_ref[core, g, 8 * tiles : height] = gram


def last_product(parts_ref, transport_ref, out_ref, sketch_ref):
    cores, chips, _, _ = out_ref.shape
    sketch, gram, columns = product(parts_ref, transport_ref)
    sketch_ref[...] = sketch
    lane = lanes_of((8, 128))
    low_half, even = lane < 64, lane % 64 < 32
    for wide in range(chips // 8):
        block = columns(512 * wide, 512)
        for c in range(4):
            t = [block[8 * a : 8 * a + 8, 128 * c : 128 * c + 128] for a in range(4)]
            u = [None] * 4
            for a in (0, 1):
                u[a] = jnp.where(low_half, t[a], pltpu.roll(t[a + 2], 64, axis=1))
                u[a + 2] = jnp.where(low_half, pltpu.roll(t[a], 64, axis=1), t[a + 2])
            for a in (0, 2):
                v0 = jnp.where(even, u[a], pltpu.roll(u[a + 1], 32, axis=1))
                v1 = jnp.where(even, pltpu.roll(u[a], 96, axis=1), u[a + 1])
                for b, v in ((a, v0), (a + 1, v1)):
                    device = 16 * wide + 4 * c + b
                    out_ref[device % 2, device // 2, 0:8] = v
    for core in range(cores):
        for chip in range(chips):
            out_ref[core, chip, 8:16] = gram


def normalise(total_rows, sums_ref, out_ref):
    peers, height, _ = sums_ref.shape
    total = sums_ref[0]
    for p in range(1, peers):
        total = total + sums_ref[p]
    tiles = height // 8 - 1
    inverse = inverse_factor(unpack_square(total[8 * tiles :]) / total_rows)
    for c in range(tiles // 4):
        block = total[32 * c : 32 * c + 32]
        panel = jnp.dot(inverse, block, precision=HIGHEST, preferred_element_type=F32).astype(BF16)
        for copy in range(out_ref.shape[0]):
            out_ref[copy, :, 128 * c : 128 * c + 128] = panel


def finish(total_rows, sums_ref, sketch_ref, basis_ref, coimage_ref):
    total = sums_ref[0]
    for p in range(1, sums_ref.shape[0]):
        total = total + sums_ref[p]
    inverse = inverse_factor(unpack_square(total[8:16]) / total_rows)
    basis_ref[...] = jnp.dot(
        inverse, sketch_ref[...], precision=HIGHEST, preferred_element_type=F32
    )
    block = unpack_square(total[0:8])[:, :RANK]
    coimage_ref[...] = lax.dot_general(
        block, inverse, (((0,), (1,)), ((), ())), precision=HIGHEST, preferred_element_type=F32
    )


def on_device(transport, test_panel):
    rows, cols = transport.shape
    total_rows = rows * lax.axis_size(("y", "z", "core"))
    ny, nz, nx = (lax.axis_size(name) for name in ("y", "z", "x"))
    chips = ny * nz
    flops = 2 * rows * cols * 128
    shape = jax.ShapeDtypeStruct

    halves = [test_panel[:16], test_panel[16:]]
    tile = jnp.concatenate(halves + halves, axis=1)
    other = lax.ppermute(tile, "core", [(0, 1), (1, 0)])
    mine = (lanes_of((16, 128)) < 64) == (lax.axis_index("core") == 0)
    pair = jnp.where(mine, tile, other)
    tiles = lax.all_to_all(jnp.broadcast_to(pair, (chips, 16, 128)), CHIPS, 0, 0)
    partial = kernel_call(
        first_sketch, shape((nx, RANK, rows), F32), flops, 5 << 20, tiles, transport
    )
    parts = lax.all_to_all(partial, "x", 0, 0)

    width = cols // (2 * nz)
    height = RANK * width // 128 + 8
    sums = kernel_call(
        middle_product, shape((2, nz, height, 128), F32), flops, 5 << 20, parts, transport
    )
    sums = jnp.sum(lax.all_to_all(sums, "core", 0, 0), axis=0)
    sums = jnp.sum(lax.all_to_all(sums, "z", 0, 0), axis=0)
    sums = lax.all_to_all(jnp.broadcast_to(sums, (ny, height, 128)), "y", 0, 0)
    panel = kernel_call(
        functools.partial(normalise, total_rows), shape((nz, RANK, width), BF16), 1 << 20, 1 << 20, sums
    )
    panel = lax.all_to_all(panel, "z", 0, 0)
    panel = lax.all_to_all(jnp.broadcast_to(panel, (2, nz, RANK, width)), "core", 0, 0)
    partial = kernel_call(
        next_sketch,
        shape((nx, RANK, rows), F32),
        flops,
        5 << 20,
        panel.reshape(2 * nz, RANK, width),
        transport,
    )
    parts = lax.all_to_all(partial, "x", 0, 0)

    sums, sketch = kernel_call(
        last_product,
        (shape((2, chips, 16, 128), F32), shape((RANK, rows), F32)),
        flops,
        6 << 20,
        parts,
        transport,
    )
    sums = jnp.sum(lax.all_to_all(sums, "core", 0, 0), axis=0)
    sums = lax.all_to_all(sums, CHIPS, 0, 0)
    basis, coimage = kernel_call(
        functools.partial(finish, total_rows),
        (shape((RANK, rows), F32), shape((RANK, RANK), F32)),
        1 << 20,
        1 << 20,
        sums,
        sketch,
    )
    return (basis.T, coimage)


def solution(mesh):
    sizes = {"cam": (("y", 8), ("z", 8), ("core", 2)), "proj": (("x", 4),)}
    names = [name for axis in mesh.axis_names for name, _ in sizes[axis]]
    shape = [size for axis in mesh.axis_names for _, size in sizes[axis]]
    fine = Mesh(np.asarray(mesh.devices).reshape(shape), names)
    rows = ("y", "z", "core")
    return jax.shard_map(
        on_device,
        mesh=fine,
        in_specs=(P(rows, "x"), P(("x",) + rows, None)),
        out_specs=(P(rows, None), P(("x",) + rows, None)),
        check_vma=False,
    )
```

time: 1630 us -> 148 us (0.09)
  blocking collectives: 1100 us -> 128 us
  waiting for transfers between devices: 481 us -> 1.11 us
  matrix products: 18.9 us -> 0 us
    psum x2 -> x0, blocking collectives: 989 us -> none  [on_device(): gram = lax.psum(small_gram(sketch), 'cam') / total_rows]
    unnamed x6 -> x0, waiting for transfers between devices: 386 us -> none
    all_to_all x0 -> x10, blocking collectives: none -> 128 us  [the longest x1 31.7 us: on_device(): lax.all_to_all(jnp.broadcast_to(pair, (chips, 16, 128)), CHIPS, 0, 0)]
    all_gather x2 -> x0, blocking collectives: 107 us -> none  [on_device(): lax.all_gather(panel_piece, 'cam', axis=0, tiled=True)]
    psum x2 -> x0, waiting for transfers between devices: 94.3 us -> none  [on_device(): sketch = lax.psum(partial_sketch, 'proj')]
    dot_general x6 -> x0, matrix products: 16.6 us -> none  [the longest x2 8.39 us: on_device(): jnp.dot(transport, lax.all_gather(panel_piece, 'cam', axis=0, tiled=True)...]
  transfers between devices with their start and end apart: 4 -> 1, of which waited for: 4 -> 1; matrix products, arithmetic and copies ran while one was open for 0% -> 0% of each run, Pallas kernels for 0% -> 0%
where the time goes in v2:
time: 148 us; the launch traced here: 145 us
  blocking collectives  128 us (86%)
  Pallas kernels  7.4 us (5%)
  local copies, waits for them, and re-layouts  5.16 us (3%)
  starting transfers between devices  1.91 us (1%)
    all_to_all x1, blocking collectives, on_device(): lax.all_to_all(jnp.broadcast_to(pair, (chips, 16, 128)), CHIPS, 0, 0)  31.7 us
    all_to_all x1, blocking collectives, on_device(): sums = lax.all_to_all(sums, CHIPS, 0, 0)  23.2 us
    all_to_all x2, blocking collectives, on_device(): parts = lax.all_to_all(partial, 'x', 0, 0)  18.8 us
    all_to_all x1, blocking collectives, on_device(): sums = jnp.sum(lax.all_to_all(sums, 'z', 0, 0), axis=0)  15.5 us
    all_to_all x1, blocking collectives, on_device(): sums = lax.all_to_all(jnp.broadcast_to(sums, (ny, height, 128)), 'y', 0, 0)  15.1 us
    all_to_all x1, blocking collectives, on_device(): panel = lax.all_to_all(panel, 'z', 0, 0)  11.5 us
    all_to_all x2, blocking collectives, on_device(): sums = jnp.sum(lax.all_to_all(sums, 'core', 0, 0), axis=0)  8.78 us
    pallas_call x6, Pallas kernels, kernel_call(): pl.pallas_call(body, out_shape=outs, in_specs=[VMEM] * len(args), out_spe...  7.4 us
  transfers between devices with their start and end apart: 1, of which 1 were waited for; matrix products, arithmetic and copies ran while one was open for 0% of the time, Pallas kernels for 0%

profile of v2, /device:TPU:6, one launch (start us, length us, event | category | flops | bytes accessed | tf_op | source)
XLA Modules:
  0.0 145.1 jit_solution(8378606177011884113)
XLA Ops:
  0.6 0.7 fusion
  1.3 0.1 pad_maximum_fusion
  1.4 1.9 %collective-permute-start = (bf16[16,128]{1,0:T(8,128)(2,1)S(1)}, bf16[16,128]{1,0:T(8,128)(2,1)S(1)}, u32[]{:S(2)}, u32[]{:S(2)}) collective-permute-start(bf16[16,128]{1,0:T(8,128)(2,1)S(1)} %pad_maximum_fusion), channel_id=1, source_target_pairs={{0,4},{4,0},{1,5},{5,1},{2,6},{6,2},{3,7},{7,3},{8,12},{12,8},{9,1... | collective-permute-start | bytes 12296 | tf_op jit(solution)/shard_map/ppermute | solution.py:200
  3.4 1.1 collective-permute-done
  4.5 0.1 broadcast_select_fusion
  4.6 31.7 %all_to_all.50.tiles_ref = bf16[64,16,128]{2,1,0:T(8,128)(2,1)S(1)} all-to-all(bf16[64,16,128]{2,1,0:T(8,128)(2,1)S(1)} %broadcast_in_dim.9), channel_id=1, replica_groups=mesh['y'=8,'z'=8,'core'=2,'x'=4] {'y','z'}, dimensions={0} | all-to-all | bytes 524288 | tf_op jit(solution)/shard_map/all_to_all | solution.py:203
  36.3 0.0 copy-start
  36.3 2.2 %copy-done = bf16[512,4096]{1,0:T(8,128)(2,1)S(1)} copy-done((bf16[512,4096]{1,0:T(8,128)(2,1)S(1)}, bf16[512,4096]{1,0:T(8,128)(2,1)}, u32[]{:S(2)}) %copy-start) | copy-done | bytes 4194328
  38.5 0.0 copy-start.1
  38.5 1.3 shard_map.41
  39.8 9.2 %all_to_all.51.parts_ref = f32[4,32,512]{2,1,0:T(8,128)S(1)} all-to-all(f32[4,32,512]{2,1,0:T(8,128)S(1)} %shard_map.41), channel_id=1, replica_groups=mesh['y'=8,'z'=8,'core'=2,'x'=4] {'x'}, dimensions={0} | all-to-all | bytes 524288 | tf_op jit(solution)/shard_map/all_to_all | solution.py:207
  49.0 0.0 copy-done.1
  49.0 0.9 shard_map.42
  49.9 4.2 %all_to_all.52 = f32[2,8,72,128]{3,2,1,0:T(8,128)S(1)} all-to-all(f32[2,8,72,128]{3,2,1,0:T(8,128)S(1)} %shard_map.42), channel_id=1, replica_groups=mesh['y'=8,'z'=8,'core'=2,'x'=4] {'core'}, dimensions={0} | all-to-all | bytes 1179648 | tf_op jit(solution)/shard_map/all_to_all | solution.py:214
  54.1 15.5 %all_to_all.53 = f32[8,72,128]{2,1,0:T(8,128)S(1)} all-to-all(f32[8,72,128]{2,1,0:T(8,128)S(1)} %reduce_sum.27), channel_id=1, replica_groups=mesh['y'=8,'z'=8,'core'=2,'x'=4] {'z'}, dimensions={0} | all-to-all | bytes 589824 | tf_op jit(solution)/shard_map/all_to_all | solution.py:215
  69.7 15.1 %all_to_all.54.sums_ref = f32[8,72,128]{2,1,0:T(8,128)S(1)} all-to-all(f32[8,72,128]{2,1,0:T(8,128)S(1)} %broadcast_in_dim.10), channel_id=1, replica_groups=mesh['y'=8,'z'=8,'core'=2,'x'=4] {'y'}, dimensions={0} | all-to-all | bytes 589824 | tf_op jit(solution)/shard_map/all_to_all | solution.py:216
  84.8 1.0 shard_map.43
  85.8 11.5 %all_to_all.55 = bf16[8,32,256]{2,1,0:T(8,128)(2,1)S(1)} all-to-all(bf16[8,32,256]{2,1,0:T(8,128)(2,1)S(1)} %shard_map.43), channel_id=1, replica_groups=mesh['y'=8,'z'=8,'core'=2,'x'=4] {'z'}, dimensions={0} | all-to-all | bytes 262144 | tf_op jit(solution)/shard_map/all_to_all | solution.py:220
  97.3 3.9 %all_to_all.56 = bf16[2,8,32,256]{3,2,1,0:T(8,128)(2,1)S(1)} all-to-all(bf16[2,8,32,256]{3,2,1,0:T(8,128)(2,1)S(1)} %broadcast_in_dim.11), channel_id=1, replica_groups=mesh['y'=8,'z'=8,'core'=2,'x'=4] {'core'}, dimensions={0} | all-to-all | bytes 524288 | tf_op jit(solution)/shard_map/all_to_all | solution.py:221
  101.2 0.0 copy-start.2
  101.2 2.2 %copy-done.2 = bf16[512,4096]{1,0:T(8,128)(2,1)S(1)} copy-done((bf16[512,4096]{1,0:T(8,128)(2,1)S(1)}, bf16[512,4096]{1,0:T(8,128)(2,1)}, u32[]{:S(2)}) %copy-start.2) | copy-done | bytes 4194328
  103.4 1.4 shard_map.44
  104.8 9.6 %all_to_all.57.parts_ref = f32[4,32,512]{2,1,0:T(8,128)S(1)} all-to-all(f32[4,32,512]{2,1,0:T(8,128)S(1)} %shard_map.44), channel_id=1, replica_groups=mesh['y'=8,'z'=8,'core'=2,'x'=4] {'x'}, dimensions={0} | all-to-all | bytes 524288 | tf_op jit(solution)/shard_map/all_to_all | solution.py:230
  114.4 1.1 shard_map.45
  115.5 4.6 %all_to_all.58 = f32[2,64,16,128]{3,2,1,0:T(8,128)S(1)} all-to-all(f32[2,64,16,128]{3,2,1,0:T(8,128)S(1)} %get-tuple-element.6), channel_id=1, replica_groups=mesh['y'=8,'z'=8,'core'=2,'x'=4] {'core'}, dimensions={0} | all-to-all | bytes 2097152 | tf_op jit(solution)/shard_map/all_to_all | solution.py:240
  120.1 0.1 reduce_sum.29
  120.2 23.2 %all_to_all.59.sums_ref = f32[64,16,128]{2,1,0:T(8,128)S(1)} all-to-all(f32[64,16,128]{2,1,0:T(8,128)S(1)} %reduce_sum.29), channel_id=1, replica_groups=mesh['y'=8,'z'=8,'core'=2,'x'=4] {'y','z'}, dimensions={0} | all-to-all | bytes 1048576 | tf_op jit(solution)/shard_map/all_to_all | solution.py:241
  143.4 1.8 %shard_map.46 = (f32[32,512]{1,0:T(8,128)}, f32[32,32]{1,0:T(8,128)}) custom-call(f32[64,16,128]{2,1,0:T(8,128)S(1)} %all_to_all.59.sums_ref, f32[32,512]{1,0:T(8,128)S(1)} %get-tuple-element.7.sketch_ref), custom_call_target="tpu_custom_call" | custom-call | flops 1048576 | bytes 1048576 | tf_op jit(solution)/shard_map/pallas_call | solution.py:23
  (6 shorter events, 0.1 us)
Async XLA Ops:
  1.4 3.0 %collective-permute-start = (bf16[16,128]{1,0:T(8,128)(2,1)S(1)}, bf16[16,128]{1,0:T(8,128)(2,1)S(1)}, u32[]{:S(2)}, u32[]{:S(2)}) collective-permute-start(bf16[16,128]{1,0:T(8,128)(2,1)S(1)} %pad_maximum_fusion), channel_id=1, source_target_pairs={{0,4},{4,0},{1,5},{5,1},{2,6},{6,2},{3,7},{7,3},{8,12},{12,8},{9,1... | collective-permute-start | bytes 12296 | tf_op jit(solution)/shard_map/ppermute | solution.py:200
  36.3 2.2 %copy-start = (bf16[512,4096]{1,0:T(8,128)(2,1)S(1)}, bf16[512,4096]{1,0:T(8,128)(2,1)}, u32[]{:S(2)}) copy-start(bf16[512,4096]{1,0:T(8,128)(2,1)} %transport_ref.7) | copy-start | bytes 12582916
  38.5 10.5 %copy-start.1 = (bf16[512,4096]{1,0:T(8,128)(2,1)S(1)}, bf16[512,4096]{1,0:T(8,128)(2,1)}, u32[]{:S(2)}) copy-start(bf16[512,4096]{1,0:T(8,128)(2,1)} %transport_ref.7) | copy-start | bytes 12582916
  101.2 2.2 %copy-start.2 = (bf16[512,4096]{1,0:T(8,128)(2,1)S(1)}, bf16[512,4096]{1,0:T(8,128)(2,1)}, u32[]{:S(2)}) copy-start(bf16[512,4096]{1,0:T(8,128)(2,1)} %transport_ref.7) | copy-start | bytes 12582916

commit v3 on v2

--- a/solution.py
+++ b/solution.py
@@ -19,13 +19,22 @@
 TN = (((0,), (0,)), ((), ()))
 
 
-def kernel_call(body, outs, flops, moved, *args):
+def kernel_call(body, outs, flops, moved, *args, streamed=None):
+    specs, scratch = [VMEM] * len(args), []
+    if streamed:
+        specs[-1] = pl.BlockSpec(memory_space=pltpu.HBM)
+        rows, cols = args[-1].shape
+        scratch = [
+            pltpu.VMEM((streamed, rows, cols // streamed), args[-1].dtype),
+            pltpu.SemaphoreType.DMA((streamed,)),
+        ]
     return pl.pallas_call(
         body,
         out_shape=outs,
-        in_specs=[VMEM] * len(args),
+        in_specs=specs,
         out_specs=jax.tree.map(lambda _: VMEM, outs),
-        compiler_params=pltpu.CompilerParams(vmem_limit_bytes=24 << 20),
+        scratch_shapes=scratch,
+        compiler_params=pltpu.CompilerParams(vmem_limit_bytes=(51 if streamed else 24) << 20),
         cost_estimate=pl.CostEstimate(flops=flops, bytes_accessed=moved, transcendentals=0),
     )(*args)
 
@@ -68,44 +77,57 @@
     return (work / jnp.sqrt(pivots))[:, RANK : 2 * RANK]
 
 
-def first_sketch(tiles_ref, transport_ref, out_ref):
-    chips, cols = tiles_ref.shape[0], transport_ref.shape[1]
+def stream(source_ref, blocks_ref, semaphores):
+    width = blocks_ref.shape[2]
+    copies = [
+        pltpu.make_async_copy(
+            source_ref.at[:, i * width : (i + 1) * width], blocks_ref.at[i], semaphores.at[i]
+        )
+        for i in range(blocks_ref.shape[0])
+    ]
+    for copy in copies:
+        copy.start()
+
+    def block(i):
+        copies[i].wait()
+        return blocks_ref[i]
+
+    return block
+
+
+def first_sketch(tiles_ref, transport_ref, out_ref, blocks_ref, semaphores):
+    block = stream(transport_ref, blocks_ref, semaphores)
+    chips, blocks = tiles_ref.shape[0], blocks_ref.shape[0]
     lane = lanes_of((16, 128))
     masks = [(lane >= 32 * q) & (lane < 32 * q + 32) for q in range(4)]
     total = jnp.zeros((transport_ref.shape[0], 128), F32)
-    group = 8
-    for start in range(0, chips, group):
+    group = chips // blocks
+    for i in range(blocks):
         rows = []
-        for chip in range(start, start + group):
+        for chip in range(i * group, (i + 1) * group):
             tile = tiles_ref[chip]
             rows += [jnp.where(mask, tile, jnp.zeros_like(tile)) for mask in masks]
-        at = start * (cols // chips)
-        total += jnp.dot(
-            transport_ref[:, at : at + group * (cols // chips)],
-            jnp.concatenate(rows),
-            preferred_element_type=F32,
-        )
+        total += jnp.dot(block(i), jnp.concatenate(rows), preferred_element_type=F32)
     turned = total.T
     sketch = (turned[0:32] + turned[32:64]) + (turned[64:96] + turned[96:128])
     for copy in range(out_ref.shape[0]):
         out_ref[copy] = sketch
 
 
-def next_sketch(panel_ref, transport_ref, out_ref):
-    groups, _, width = panel_ref.shape
+def next_sketch(panel_ref, transport_ref, out_ref, blocks_ref, semaphores):
+    block = stream(transport_ref, blocks_ref, semaphores)
+    groups, blocks = panel_ref.shape[0], blocks_ref.shape[0]
+    each = groups // blocks
     sketch = jnp.zeros((RANK, transport_ref.shape[0]), F32)
-    for g in range(groups):
-        sketch += lax.dot_general(
-            panel_ref[g],
-            transport_ref[:, g * width : (g + 1) * width],
-            NT,
-            preferred_element_type=F32,
-        )
+    for i in range(blocks):
+        panel = jnp.concatenate([panel_ref[i * each + g] for g in range(each)], axis=1)
+        sketch += lax.dot_general(panel, block(i), NT, preferred_element_type=F32)
     for copy in range(out_ref.shape[0]):
         out_ref[copy] = sketch
 
 
-def product(parts_ref, transport_ref):
+def product(parts_ref, transport_ref, blocks_ref, semaphores):
+    block = stream(transport_ref, blocks_ref, semaphores)
     sketch = (parts_ref[0] + parts_ref[1]) + (parts_ref[2] + parts_ref[3])
     gram = lax.dot_general(sketch, sketch, NT, precision=HIGHEST, preferred_element_type=F32)
     gram = jnp.concatenate([gram, jnp.zeros((RANK, 128 - RANK), F32)], axis=1)
@@ -113,35 +135,39 @@
     low = (sketch - high.astype(F32)).astype(BF16)
     both = jnp.concatenate([high, low])
 
-    def columns(at, width):
-        out = jnp.dot(both, transport_ref[:, at : at + width], preferred_element_type=F32)
+    def columns(i):
+        out = jnp.dot(both, block(i), preferred_element_type=F32)
         return out[:RANK] + out[RANK:]
 
     return sketch, pack_square(gram), columns
 
 
-def middle_product(parts_ref, transport_ref, out_ref):
+def middle_product(parts_ref, transport_ref, out_ref, blocks_ref, semaphores):
     cores, groups, height, _ = out_ref.shape
     tiles = height // 8 - 1
-    width = tiles // 4 * 128
-    _, gram, columns = product(parts_ref, transport_ref)
+    each = blocks_ref.shape[2] // 128 * 4 // tiles
+    _, gram, columns = product(parts_ref, transport_ref, blocks_ref, semaphores)
     for core in range(cores):
+        for wide in range(groups // each):
+            block = columns(core * (groups // each) + wide)
+            for g in range(each):
+                for t in range(tiles):
+                    a, c = t % 4, t // 4 + g * (tiles // 4)
+                    out_ref[core, wide * each + g, 8 * t : 8 * t + 8] = block[
+                        8 * a : 8 * a + 8, 128 * c : 128 * c + 128
+                    ]
         for g in range(groups):
-            block = columns((core * groups + g) * width, width)
-            for t in range(tiles):
-                a, c = t % 4, t // 4
-                out_ref[core, g, 8 * t : 8 * t + 8] = block[8 * a : 8 * a + 8, 128 * c : 128 * c + 128]
             out_ref[core, g, 8 * tiles : height] = gram
 
 
-def last_product(parts_ref, transport_ref, out_ref, sketch_ref):
+def last_product(parts_ref, transport_ref, out_ref, sketch_ref, blocks_ref, semaphores):
     cores, chips, _, _ = out_ref.shape
-    sketch, gram, columns = product(parts_ref, transport_ref)
+    sketch, gram, columns = product(parts_ref, transport_ref, blocks_ref, semaphores)
     sketch_ref[...] = sketch
     lane = lanes_of((8, 128))
     low_half, even = lane < 64, lane % 64 < 32
     for wide in range(chips // 8):
-        block = columns(512 * wide, 512)
+        block = columns(wide)
         for c in range(4):
             t = [block[8 * a : 8 * a + 8, 128 * c : 128 * c + 128] for a in range(4)]
             u = [None] * 4
@@ -202,14 +228,20 @@
     pair = jnp.where(mine, tile, other)
     tiles = lax.all_to_all(jnp.broadcast_to(pair, (chips, 16, 128)), CHIPS, 0, 0)
     partial = kernel_call(
-        first_sketch, shape((nx, RANK, rows), F32), flops, 5 << 20, tiles, transport
+        first_sketch, shape((nx, RANK, rows), F32), flops, 5 << 20, tiles, transport, streamed=8
     )
     parts = lax.all_to_all(partial, "x", 0, 0)
 
     width = cols // (2 * nz)
     height = RANK * width // 128 + 8
     sums = kernel_call(
-        middle_product, shape((2, nz, height, 128), F32), flops, 5 << 20, parts, transport
+        middle_product,
+        shape((2, nz, height, 128), F32),
+        flops,
+        5 << 20,
+        parts,
+        transport,
+        streamed=8,
     )
     sums = jnp.sum(lax.all_to_all(sums, "core", 0, 0), axis=0)
     sums = jnp.sum(lax.all_to_all(sums, "z", 0, 0), axis=0)
@@ -226,6 +258,7 @@
         5 << 20,
         panel.reshape(2 * nz, RANK, width),
         transport,
+        streamed=8,
     )
     parts = lax.all_to_all(partial, "x", 0, 0)
 
@@ -236,6 +269,7 @@
         6 << 20,
         parts,
         transport,
+        streamed=8,
     )
     sums = jnp.sum(lax.all_to_all(sums, "core", 0, 0), axis=0)
     sums = lax.all_to_all(sums, CHIPS, 0, 0)

time: 148 us -> 152 us (1.027)
  Pallas kernels: 7.4 us -> 16.5 us
  local copies, waits for them, and re-layouts: 5.16 us -> 0.78 us
    pallas_call x6, Pallas kernels: 7.4 us -> 16.5 us  [kernel_call(): pl.pallas_call(body, out_shape=outs, in_specs=specs, out_specs=jax.tree.m...]
    unnamed x6 -> x0, local copies, waits for them, and re-layouts: 4.38 us -> none
where the time goes in v3:
time: 152 us; the launch traced here: 150 us
  blocking collectives  128 us (84%)
  Pallas kernels  16.5 us (11%)
  starting transfers between devices  1.91 us (1%)
    all_to_all x1, blocking collectives, on_device(): lax.all_to_all(jnp.broadcast_to(pair, (chips, 16, 128)), CHIPS, 0, 0)  31.7 us
    all_to_all x1, blocking collectives, on_device(): sums = lax.all_to_all(sums, CHIPS, 0, 0)  23.2 us
    all_to_all x2, blocking collectives, on_device(): parts = lax.all_to_all(partial, 'x', 0, 0)  18.8 us
    pallas_call x6, Pallas kernels, kernel_call(): pl.pallas_call(body, out_shape=outs, in_specs=specs, out_specs=jax.tree.m...  16.5 us
    all_to_all x1, blocking collectives, on_device(): sums = jnp.sum(lax.all_to_all(sums, 'z', 0, 0), axis=0)  15.5 us
    all_to_all x1, blocking collectives, on_device(): sums = lax.all_to_all(jnp.broadcast_to(sums, (ny, height, 128)), 'y', 0, 0)  15.1 us
    all_to_all x1, blocking collectives, on_device(): panel = lax.all_to_all(panel, 'z', 0, 0)  11.5 us
    all_to_all x2, blocking collectives, on_device(): sums = jnp.sum(lax.all_to_all(sums, 'core', 0, 0), axis=0)  8.78 us
  transfers between devices with their start and end apart: 1, of which 1 were waited for; matrix products, arithmetic and copies ran while one was open for 0% of the time, Pallas kernels for 0%

profile of v3, /device:TPU:6, one launch (start us, length us, event | category | flops | bytes accessed | tf_op | source)
XLA Modules:
  0.0 149.8 jit_solution(1216742161358621839)
XLA Ops:
  0.6 0.7 fusion
  1.3 0.1 pad_maximum_fusion
  1.4 1.9 %collective-permute-start = (bf16[16,128]{1,0:T(8,128)(2,1)S(1)}, bf16[16,128]{1,0:T(8,128)(2,1)S(1)}, u32[]{:S(2)}, u32[]{:S(2)}) collective-permute-start(bf16[16,128]{1,0:T(8,128)(2,1)S(1)} %pad_maximum_fusion), channel_id=1, source_target_pairs={{0,4},{4,0},{1,5},{5,1},{2,6},{6,2},{3,7},{7,3},{8,12},{12,8},{9,1... | collective-permute-start | bytes 12296 | tf_op jit(solution)/shard_map/ppermute | solution.py:226
  3.4 1.1 collective-permute-done
  4.5 0.1 broadcast_select_fusion
  4.6 31.7 %all_to_all.50.tiles_ref = bf16[64,16,128]{2,1,0:T(8,128)(2,1)S(1)} all-to-all(bf16[64,16,128]{2,1,0:T(8,128)(2,1)S(1)} %broadcast_in_dim.9), channel_id=1, replica_groups=mesh['y'=8,'z'=8,'core'=2,'x'=4] {'y','z'}, dimensions={0} | all-to-all | bytes 524288 | tf_op jit(solution)/shard_map/all_to_all | solution.py:229
  36.3 4.0 %shard_map.41 = f32[4,32,512]{2,1,0:T(8,128)S(1)} custom-call(bf16[64,16,128]{2,1,0:T(8,128)(2,1)S(1)} %all_to_all.50.tiles_ref, bf16[512,4096]{1,0:T(8,128)(2,1)} %transport_ref.7), custom_call_target="tpu_custom_call" | custom-call | flops 536870912 | bytes 5242880 | tf_op jit(solution)/shard_map/pallas_call | solution.py:31
  40.2 9.2 %all_to_all.51.parts_ref = f32[4,32,512]{2,1,0:T(8,128)S(1)} all-to-all(f32[4,32,512]{2,1,0:T(8,128)S(1)} %shard_map.41), channel_id=1, replica_groups=mesh['y'=8,'z'=8,'core'=2,'x'=4] {'x'}, dimensions={0} | all-to-all | bytes 524288 | tf_op jit(solution)/shard_map/all_to_all | solution.py:233
  49.4 2.9 %shard_map.42 = f32[2,8,72,128]{3,2,1,0:T(8,128)S(1)} custom-call(f32[4,32,512]{2,1,0:T(8,128)S(1)} %all_to_all.51.parts_ref, bf16[512,4096]{1,0:T(8,128)(2,1)} %transport_ref.7), custom_call_target="tpu_custom_call" | custom-call | flops 536870912 | bytes 5242880 | tf_op jit(solution)/shard_map/pallas_call | solution.py:31
  52.4 4.2 %all_to_all.52 = f32[2,8,72,128]{3,2,1,0:T(8,128)S(1)} all-to-all(f32[2,8,72,128]{3,2,1,0:T(8,128)S(1)} %shard_map.42), channel_id=1, replica_groups=mesh['y'=8,'z'=8,'core'=2,'x'=4] {'core'}, dimensions={0} | all-to-all | bytes 1179648 | tf_op jit(solution)/shard_map/all_to_all | solution.py:246
  56.6 15.5 %all_to_all.53 = f32[8,72,128]{2,1,0:T(8,128)S(1)} all-to-all(f32[8,72,128]{2,1,0:T(8,128)S(1)} %reduce_sum.27), channel_id=1, replica_groups=mesh['y'=8,'z'=8,'core'=2,'x'=4] {'z'}, dimensions={0} | all-to-all | bytes 589824 | tf_op jit(solution)/shard_map/all_to_all | solution.py:247
  72.2 15.1 %all_to_all.54.sums_ref = f32[8,72,128]{2,1,0:T(8,128)S(1)} all-to-all(f32[8,72,128]{2,1,0:T(8,128)S(1)} %broadcast_in_dim.10), channel_id=1, replica_groups=mesh['y'=8,'z'=8,'core'=2,'x'=4] {'y'}, dimensions={0} | all-to-all | bytes 589824 | tf_op jit(solution)/shard_map/all_to_all | solution.py:248
  87.3 1.0 shard_map.43
  88.3 11.5 %all_to_all.55 = bf16[8,32,256]{2,1,0:T(8,128)(2,1)S(1)} all-to-all(bf16[8,32,256]{2,1,0:T(8,128)(2,1)S(1)} %shard_map.43), channel_id=1, replica_groups=mesh['y'=8,'z'=8,'core'=2,'x'=4] {'z'}, dimensions={0} | all-to-all | bytes 262144 | tf_op jit(solution)/shard_map/all_to_all | solution.py:252
  99.8 3.9 %all_to_all.56 = bf16[2,8,32,256]{3,2,1,0:T(8,128)(2,1)S(1)} all-to-all(bf16[2,8,32,256]{3,2,1,0:T(8,128)(2,1)S(1)} %broadcast_in_dim.11), channel_id=1, replica_groups=mesh['y'=8,'z'=8,'core'=2,'x'=4] {'core'}, dimensions={0} | all-to-all | bytes 524288 | tf_op jit(solution)/shard_map/all_to_all | solution.py:253
  103.7 2.7 %shard_map.44 = f32[4,32,512]{2,1,0:T(8,128)S(1)} custom-call(bf16[16,32,256]{2,1,0:T(8,128)(2,1)S(1)} %bitcast.2, bf16[512,4096]{1,0:T(8,128)(2,1)} %transport_ref.7), custom_call_target="tpu_custom_call" | custom-call | flops 536870912 | bytes 5242880 | tf_op jit(solution)/shard_map/pallas_call | solution.py:31
  106.4 9.6 %all_to_all.57.parts_ref = f32[4,32,512]{2,1,0:T(8,128)S(1)} all-to-all(f32[4,32,512]{2,1,0:T(8,128)S(1)} %shard_map.44), channel_id=1, replica_groups=mesh['y'=8,'z'=8,'core'=2,'x'=4] {'x'}, dimensions={0} | all-to-all | bytes 524288 | tf_op jit(solution)/shard_map/all_to_all | solution.py:263
  116.0 4.1 %shard_map.45 = (f32[2,64,16,128]{3,2,1,0:T(8,128)S(1)}, f32[32,512]{1,0:T(8,128)S(1)}) custom-call(f32[4,32,512]{2,1,0:T(8,128)S(1)} %all_to_all.57.parts_ref, bf16[512,4096]{1,0:T(8,128)(2,1)} %transport_ref.7), custom_call_target="tpu_custom_call" | custom-call | flops 536870912 | bytes 6291456 | tf_op jit(solution)/shard_map/pallas_call | solution.py:31
  120.2 4.6 %all_to_all.58 = f32[2,64,16,128]{3,2,1,0:T(8,128)S(1)} all-to-all(f32[2,64,16,128]{3,2,1,0:T(8,128)S(1)} %get-tuple-element.6), channel_id=1, replica_groups=mesh['y'=8,'z'=8,'core'=2,'x'=4] {'core'}, dimensions={0} | all-to-all | bytes 2097152 | tf_op jit(solution)/shard_map/all_to_all | solution.py:274
  124.8 0.1 reduce_sum.29
  124.9 23.2 %all_to_all.59.sums_ref = f32[64,16,128]{2,1,0:T(8,128)S(1)} all-to-all(f32[64,16,128]{2,1,0:T(8,128)S(1)} %reduce_sum.29), channel_id=1, replica_groups=mesh['y'=8,'z'=8,'core'=2,'x'=4] {'y','z'}, dimensions={0} | all-to-all | bytes 1048576 | tf_op jit(solution)/shard_map/all_to_all | solution.py:275
  148.1 1.8 %shard_map.46 = (f32[32,512]{1,0:T(8,128)}, f32[32,32]{1,0:T(8,128)}) custom-call(f32[64,16,128]{2,1,0:T(8,128)S(1)} %all_to_all.59.sums_ref, f32[32,512]{1,0:T(8,128)S(1)} %get-tuple-element.7.sketch_ref), custom_call_target="tpu_custom_call" | custom-call | flops 1048576 | bytes 1048576 | tf_op jit(solution)/shard_map/pallas_call | solution.py:31
  (6 shorter events, 0.1 us)
Async XLA Ops:
  1.4 3.0 %collective-permute-start = (bf16[16,128]{1,0:T(8,128)(2,1)S(1)}, bf16[16,128]{1,0:T(8,128)(2,1)S(1)}, u32[]{:S(2)}, u32[]{:S(2)}) collective-permute-start(bf16[16,128]{1,0:T(8,128)(2,1)S(1)} %pad_maximum_fusion), channel_id=1, source_target_pairs={{0,4},{4,0},{1,5},{5,1},{2,6},{6,2},{3,7},{7,3},{8,12},{12,8},{9,1... | collective-permute-start | bytes 12296 | tf_op jit(solution)/shard_map/ppermute | solution.py:226

commit v4 on v2

--- a/solution.py
+++ b/solution.py
@@ -66,6 +66,11 @@
                 columns[later] = columns[later] - factor * columns[later][k : k + 1]
             work = work - factor * work[k : k + 1]
     return (work / jnp.sqrt(pivots))[:, RANK : 2 * RANK]
+
+
+def fan_out(pair_ref, out_ref):
+    for copy in range(out_ref.shape[0]):
+        out_ref[copy] = pair_ref[...]
 
 
 def first_sketch(tiles_ref, transport_ref, out_ref):
@@ -200,7 +205,8 @@
     other = lax.ppermute(tile, "core", [(0, 1), (1, 0)])
     mine = (lanes_of((16, 128)) < 64) == (lax.axis_index("core") == 0)
     pair = jnp.where(mine, tile, other)
-    tiles = lax.all_to_all(jnp.broadcast_to(pair, (chips, 16, 128)), CHIPS, 0, 0)
+    copies = kernel_call(fan_out, shape((chips, 16, 128), BF16), 1 << 32, 8 << 20, pair)
+    tiles = lax.all_to_all(copies, CHIPS, 0, 0)
     partial = kernel_call(
         first_sketch, shape((nx, RANK, rows), F32), flops, 5 << 20, tiles, transport
     )
@@ -215,7 +221,7 @@
     sums = jnp.sum(lax.all_to_all(sums, "z", 0, 0), axis=0)
     sums = lax.all_to_all(jnp.broadcast_to(sums, (ny, height, 128)), "y", 0, 0)
     panel = kernel_call(
-        functools.partial(normalise, total_rows), shape((nz, RANK, width), BF16), 1 << 20, 1 << 20, sums
+        functools.partial(normalise, total_rows), shape((nz, RANK, width), BF16), 1 << 32, 8 << 20, sums
     )
     panel = lax.all_to_all(panel, "z", 0, 0)
     panel = lax.all_to_all(jnp.broadcast_to(panel, (2, nz, RANK, width)), "core", 0, 0)

time: 148 us -> 144 us (0.973)
  local copies, waits for them, and re-layouts: 5.16 us -> 0.75 us
    unnamed x6 -> x4, local copies, waits for them, and re-layouts: 4.38 us -> 0.01 us
    pallas_call x6 -> x7, Pallas kernels: 7.4 us -> 7.44 us  [kernel_call(): pl.pallas_call(body, out_shape=outs, in_specs=[VMEM] * len(args), out_spe...]
where the time goes in v4:
time: 144 us; the launch traced here: 141 us
  blocking collectives  129 us (90%)
  Pallas kernels  7.44 us (5%)
  starting transfers between devices  1.91 us (1%)
    all_to_all x1, blocking collectives, on_device(): tiles = lax.all_to_all(copies, CHIPS, 0, 0)  31.9 us
    all_to_all x1, blocking collectives, on_device(): sums = lax.all_to_all(sums, CHIPS, 0, 0)  23.2 us
    all_to_all x2, blocking collectives, on_device(): parts = lax.all_to_all(partial, 'x', 0, 0)  18.8 us
    all_to_all x1, blocking collectives, on_device(): sums = jnp.sum(lax.all_to_all(sums, 'z', 0, 0), axis=0)  15.5 us
    all_to_all x1, blocking collectives, on_device(): sums = lax.all_to_all(jnp.broadcast_to(sums, (ny, height, 128)), 'y', 0, 0)  15.1 us
    all_to_all x1, blocking collectives, on_device(): panel = lax.all_to_all(panel, 'z', 0, 0)  11.6 us
    all_to_all x2, blocking collectives, on_device(): sums = jnp.sum(lax.all_to_all(sums, 'core', 0, 0), axis=0)  8.78 us
    pallas_call x7, Pallas kernels, kernel_call(): pl.pallas_call(body, out_shape=outs, in_specs=[VMEM] * len(args), out_spe...  7.44 us
  transfers between devices with their start and end apart: 1, of which 1 were waited for; matrix products, arithmetic and copies ran while one was open for 0% of the time, Pallas kernels for 0%

profile of v4, /device:TPU:6, one launch (start us, length us, event | category | flops | bytes accessed | tf_op | source)
XLA Modules:
  0.0 141.1 jit_solution(9094788683234586990)
XLA Ops:
  0.6 0.7 fusion
  1.3 0.1 pad_maximum_fusion
  1.4 1.9 %collective-permute-start = (bf16[16,128]{1,0:T(8,128)(2,1)S(1)}, bf16[16,128]{1,0:T(8,128)(2,1)S(1)}, u32[]{:S(2)}, u32[]{:S(2)}) collective-permute-start(bf16[16,128]{1,0:T(8,128)(2,1)S(1)} %pad_maximum_fusion), channel_id=1, source_target_pairs={{0,4},{4,0},{1,5},{5,1},{2,6},{6,2},{3,7},{7,3},{8,12},{12,8},{9,1... | collective-permute-start | bytes 12296 | tf_op jit(solution)/shard_map/ppermute | solution.py:205
  3.4 1.1 collective-permute-done
  4.5 0.1 broadcast_select_fusion.pair_ref
  4.5 0.0 copy-start
  4.6 31.9 %all_to_all.50.tiles_ref = bf16[64,16,128]{2,1,0:T(8,128)(2,1)S(1)} all-to-all(bf16[64,16,128]{2,1,0:T(8,128)(2,1)S(1)} %shard_map.41), channel_id=1, replica_groups=mesh['y'=8,'z'=8,'core'=2,'x'=4] {'y','z'}, dimensions={0} | all-to-all | bytes 524288 | tf_op jit(solution)/shard_map/all_to_all | solution.py:209
  36.5 0.0 copy-done
  36.5 1.3 shard_map.42
  37.9 9.2 %all_to_all.51.parts_ref = f32[4,32,512]{2,1,0:T(8,128)S(1)} all-to-all(f32[4,32,512]{2,1,0:T(8,128)S(1)} %shard_map.42), channel_id=1, replica_groups=mesh['y'=8,'z'=8,'core'=2,'x'=4] {'x'}, dimensions={0} | all-to-all | bytes 524288 | tf_op jit(solution)/shard_map/all_to_all | solution.py:213
  47.0 0.9 shard_map.43
  47.9 4.2 %all_to_all.52 = f32[2,8,72,128]{3,2,1,0:T(8,128)S(1)} all-to-all(f32[2,8,72,128]{3,2,1,0:T(8,128)S(1)} %shard_map.43), channel_id=1, replica_groups=mesh['y'=8,'z'=8,'core'=2,'x'=4] {'core'}, dimensions={0} | all-to-all | bytes 1179648 | tf_op jit(solution)/shard_map/all_to_all | solution.py:220
  52.2 15.5 %all_to_all.53 = f32[8,72,128]{2,1,0:T(8,128)S(1)} all-to-all(f32[8,72,128]{2,1,0:T(8,128)S(1)} %reduce_sum.27), channel_id=1, replica_groups=mesh['y'=8,'z'=8,'core'=2,'x'=4] {'z'}, dimensions={0} | all-to-all | bytes 589824 | tf_op jit(solution)/shard_map/all_to_all | solution.py:221
  67.8 15.1 %all_to_all.54.sums_ref = f32[8,72,128]{2,1,0:T(8,128)S(1)} all-to-all(f32[8,72,128]{2,1,0:T(8,128)S(1)} %broadcast_in_dim.6), channel_id=1, replica_groups=mesh['y'=8,'z'=8,'core'=2,'x'=4] {'y'}, dimensions={0} | all-to-all | bytes 589824 | tf_op jit(solution)/shard_map/all_to_all | solution.py:222
  82.8 0.0 copy-start.1
  82.8 1.0 shard_map.44
  83.9 11.6 %all_to_all.55 = bf16[8,32,256]{2,1,0:T(8,128)(2,1)S(1)} all-to-all(bf16[8,32,256]{2,1,0:T(8,128)(2,1)S(1)} %shard_map.44), channel_id=1, replica_groups=mesh['y'=8,'z'=8,'core'=2,'x'=4] {'z'}, dimensions={0} | all-to-all | bytes 262144 | tf_op jit(solution)/shard_map/all_to_all | solution.py:226
  95.5 3.9 %all_to_all.56 = bf16[2,8,32,256]{3,2,1,0:T(8,128)(2,1)S(1)} all-to-all(bf16[2,8,32,256]{3,2,1,0:T(8,128)(2,1)S(1)} %broadcast_in_dim.7), channel_id=1, replica_groups=mesh['y'=8,'z'=8,'core'=2,'x'=4] {'core'}, dimensions={0} | all-to-all | bytes 524288 | tf_op jit(solution)/shard_map/all_to_all | solution.py:227
  99.4 0.0 copy-done.1
  99.4 1.4 shard_map.45
  100.8 9.6 %all_to_all.57.parts_ref = f32[4,32,512]{2,1,0:T(8,128)S(1)} all-to-all(f32[4,32,512]{2,1,0:T(8,128)S(1)} %shard_map.45), channel_id=1, replica_groups=mesh['y'=8,'z'=8,'core'=2,'x'=4] {'x'}, dimensions={0} | all-to-all | bytes 524288 | tf_op jit(solution)/shard_map/all_to_all | solution.py:236
  110.4 1.1 shard_map.46
  111.5 4.6 %all_to_all.58 = f32[2,64,16,128]{3,2,1,0:T(8,128)S(1)} all-to-all(f32[2,64,16,128]{3,2,1,0:T(8,128)S(1)} %get-tuple-element.6), channel_id=1, replica_groups=mesh['y'=8,'z'=8,'core'=2,'x'=4] {'core'}, dimensions={0} | all-to-all | bytes 2097152 | tf_op jit(solution)/shard_map/all_to_all | solution.py:246
  116.1 0.1 reduce_sum.29
  116.2 23.2 %all_to_all.59.sums_ref = f32[64,16,128]{2,1,0:T(8,128)S(1)} all-to-all(f32[64,16,128]{2,1,0:T(8,128)S(1)} %reduce_sum.29), channel_id=1, replica_groups=mesh['y'=8,'z'=8,'core'=2,'x'=4] {'y','z'}, dimensions={0} | all-to-all | bytes 1048576 | tf_op jit(solution)/shard_map/all_to_all | solution.py:247
  139.4 1.8 %shard_map.47 = (f32[32,512]{1,0:T(8,128)}, f32[32,32]{1,0:T(8,128)}) custom-call(f32[64,16,128]{2,1,0:T(8,128)S(1)} %all_to_all.59.sums_ref, f32[32,512]{1,0:T(8,128)S(1)} %get-tuple-element.7.sketch_ref), custom_call_target="tpu_custom_call" | custom-call | flops 1048576 | bytes 1048576 | tf_op jit(solution)/shard_map/pallas_call | solution.py:23
  (6 shorter events, 0.1 us)
Async XLA Ops:
  1.4 3.0 %collective-permute-start = (bf16[16,128]{1,0:T(8,128)(2,1)S(1)}, bf16[16,128]{1,0:T(8,128)(2,1)S(1)}, u32[]{:S(2)}, u32[]{:S(2)}) collective-permute-start(bf16[16,128]{1,0:T(8,128)(2,1)S(1)} %pad_maximum_fusion), channel_id=1, source_target_pairs={{0,4},{4,0},{1,5},{5,1},{2,6},{6,2},{3,7},{7,3},{8,12},{12,8},{9,1... | collective-permute-start | bytes 12296 | tf_op jit(solution)/shard_map/ppermute | solution.py:205
  4.5 32.0 %copy-start = (bf16[512,4096]{1,0:T(8,128)(2,1)S(1)}, bf16[512,4096]{1,0:T(8,128)(2,1)}, u32[]{:S(2)}) copy-start(bf16[512,4096]{1,0:T(8,128)(2,1)} %transport_ref.7) | copy-start | bytes 12582916
  82.8 16.6 %copy-start.1 = (bf16[512,4096]{1,0:T(8,128)(2,1)S(1)}, bf16[512,4096]{1,0:T(8,128)(2,1)}, u32[]{:S(2)}) copy-start(bf16[512,4096]{1,0:T(8,128)(2,1)} %transport_ref.7) | copy-start | bytes 12582916

commit v5 on v4

--- a/solution.py
+++ b/solution.py
@@ -68,26 +68,30 @@
     return (work / jnp.sqrt(pivots))[:, RANK : 2 * RANK]
 
 
-def fan_out(pair_ref, out_ref):
+def fan_out(panel_ref, out_ref):
+    panel = jnp.concatenate([panel_ref[...].astype(F32), jnp.zeros((RANK, 128 - RANK), F32)], axis=1)
+    tile = pack_square(panel).astype(BF16)
     for copy in range(out_ref.shape[0]):
-        out_ref[copy] = pair_ref[...]
+        out_ref[copy] = tile
 
 
 def first_sketch(tiles_ref, transport_ref, out_ref):
-    chips, cols = tiles_ref.shape[0], transport_ref.shape[1]
-    lane = lanes_of((16, 128))
+    cores, chips = tiles_ref.shape[:2]
+    cols = transport_ref.shape[1]
+    lane = lanes_of((8, 128))
     masks = [(lane >= 32 * q) & (lane < 32 * q + 32) for q in range(4)]
     total = jnp.zeros((transport_ref.shape[0], 128), F32)
     group = 8
     for start in range(0, chips, group):
         rows = []
         for chip in range(start, start + group):
-            tile = tiles_ref[chip]
-            rows += [jnp.where(mask, tile, jnp.zeros_like(tile)) for mask in masks]
+            for core in range(cores):
+                tile = tiles_ref[core, chip].astype(F32)
+                rows += [jnp.where(mask, tile, 0.0) for mask in masks]
         at = start * (cols // chips)
         total += jnp.dot(
             transport_ref[:, at : at + group * (cols // chips)],
-            jnp.concatenate(rows),
+            jnp.concatenate(rows).astype(BF16),
             preferred_element_type=F32,
         )
     turned = total.T
@@ -200,37 +204,36 @@
     flops = 2 * rows * cols * 128
     shape = jax.ShapeDtypeStruct
 
-    halves = [test_panel[:16], test_panel[16:]]
-    tile = jnp.concatenate(halves + halves, axis=1)
-    other = lax.ppermute(tile, "core", [(0, 1), (1, 0)])
-    mine = (lanes_of((16, 128)) < 64) == (lax.axis_index("core") == 0)
-    pair = jnp.where(mine, tile, other)
-    copies = kernel_call(fan_out, shape((chips, 16, 128), BF16), 1 << 32, 8 << 20, pair)
+    copies = kernel_call(fan_out, shape((chips, 8, 128), BF16), 1 << 32, 8 << 20, test_panel)
     tiles = lax.all_to_all(copies, CHIPS, 0, 0)
+    tiles = lax.all_to_all(jnp.broadcast_to(tiles, (2, chips, 8, 128)), "core", 0, 0)
     partial = kernel_call(
         first_sketch, shape((nx, RANK, rows), F32), flops, 5 << 20, tiles, transport
     )
     parts = lax.all_to_all(partial, "x", 0, 0)
 
-    width = cols // (2 * nz)
+    width = cols // (2 * ny)
     height = RANK * width // 128 + 8
     sums = kernel_call(
-        middle_product, shape((2, nz, height, 128), F32), flops, 5 << 20, parts, transport
+        middle_product, shape((2, ny, height, 128), F32), flops, 5 << 20, parts, transport
     )
     sums = jnp.sum(lax.all_to_all(sums, "core", 0, 0), axis=0)
-    sums = jnp.sum(lax.all_to_all(sums, "z", 0, 0), axis=0)
-    sums = lax.all_to_all(jnp.broadcast_to(sums, (ny, height, 128)), "y", 0, 0)
+    sums = jnp.sum(lax.all_to_all(sums, "y", 0, 0), axis=0)
+    sums = lax.all_to_all(jnp.broadcast_to(sums, (nz, height, 128)), "z", 0, 0)
     panel = kernel_call(
-        functools.partial(normalise, total_rows), shape((nz, RANK, width), BF16), 1 << 32, 8 << 20, sums
-    )
-    panel = lax.all_to_all(panel, "z", 0, 0)
-    panel = lax.all_to_all(jnp.broadcast_to(panel, (2, nz, RANK, width)), "core", 0, 0)
+        functools.partial(normalise, total_rows),
+        shape((2 * ny, RANK, width), BF16),
+        1 << 32,
+        8 << 20,
+        sums,
+    )
+    panel = lax.all_to_all(panel, ("core", "y"), 0, 0)
     partial = kernel_call(
         next_sketch,
         shape((nx, RANK, rows), F32),
         flops,
         5 << 20,
-        panel.reshape(2 * nz, RANK, width),
+        panel,
         transport,
     )
     parts = lax.all_to_all(partial, "x", 0, 0)

time: 144 us -> 140 us (0.972)
  starting transfers between devices: 1.91 us -> 0 us
    all_to_all x1, blocking collectives: 31.9 us -> 29.4 us  [on_device(): tiles = lax.all_to_all(copies, CHIPS, 0, 0)]
    ppermute x1 -> x0, starting transfers between devices: 1.91 us -> none  [on_device(): other = lax.ppermute(tile, 'core', [(0, 1), (1, 0)])]
    all_to_all x4, blocking collectives: 46.1 us -> 47.7 us  [the longest x1 15.5 us: on_device(): sums = jnp.sum(lax.all_to_all(sums, 'y', 0, 0), axis=0)]
  transfers between devices with their start and end apart: 1 -> 0, of which waited for: 1 -> 0; matrix products, arithmetic and copies ran while one was open for 0% -> 0% of each run, Pallas kernels for 0% -> 0%
where the time goes in v5:
time: 140 us; the launch traced here: 138 us
  blocking collectives  129 us (92%)
  Pallas kernels  7.51 us (5%)
    all_to_all x1, blocking collectives, on_device(): tiles = lax.all_to_all(copies, CHIPS, 0, 0)  29.4 us
    all_to_all x1, blocking collectives, on_device(): sums = lax.all_to_all(sums, CHIPS, 0, 0)  24.5 us
    all_to_all x2, blocking collectives, on_device(): parts = lax.all_to_all(partial, 'x', 0, 0)  18.5 us
    all_to_all x1, blocking collectives, on_device(): sums = jnp.sum(lax.all_to_all(sums, 'y', 0, 0), axis=0)  15.5 us
    all_to_all x1, blocking collectives, on_device(): sums = lax.all_to_all(jnp.broadcast_to(sums, (nz, height, 128)), 'z', 0, 0)  15 us
    all_to_all x1, blocking collectives, on_device(): panel = lax.all_to_all(panel, ('core', 'y'), 0, 0)  13.2 us
    all_to_all x2, blocking collectives, on_device(): sums = jnp.sum(lax.all_to_all(sums, 'core', 0, 0), axis=0)  8.78 us
    pallas_call x7, Pallas kernels, kernel_call(): pl.pallas_call(body, out_shape=outs, in_specs=[VMEM] * len(args), out_spe...  7.51 us

profile of v5, /device:TPU:6, one launch (start us, length us, event | category | flops | bytes accessed | tf_op | source)
XLA Modules:
  0.0 138.0 jit_solution(18337213764391973738)
XLA Ops:
  0.6 0.0 copy-start.2
  0.6 0.7 copy-done.2
  1.3 0.0 copy-start
  1.3 0.1 shard_map.41
  1.4 29.4 %all_to_all.50 = bf16[64,8,128]{2,1,0:T(8,128)(2,1)S(1)} all-to-all(bf16[64,8,128]{2,1,0:T(8,128)(2,1)S(1)} %shard_map.41), channel_id=1, replica_groups=mesh['y'=8,'z'=8,'core'=2,'x'=4] {'y','z'}, dimensions={0} | all-to-all | bytes 262144 | tf_op jit(solution)/shard_map/all_to_all | solution.py:208
  30.8 3.9 %all_to_all.51.tiles_ref = bf16[2,64,8,128]{3,2,1,0:T(8,128)(2,1)S(1)} all-to-all(bf16[2,64,8,128]{3,2,1,0:T(8,128)(2,1)S(1)} %broadcast_in_dim.6), channel_id=1, replica_groups=mesh['y'=8,'z'=8,'core'=2,'x'=4] {'core'}, dimensions={0} | all-to-all | bytes 524288 | tf_op jit(solution)/shard_map/all_to_all | solution.py:209
  34.7 0.0 copy-done
  34.7 1.3 shard_map.42
  36.1 9.5 %all_to_all.52.parts_ref = f32[4,32,512]{2,1,0:T(8,128)S(1)} all-to-all(f32[4,32,512]{2,1,0:T(8,128)S(1)} %shard_map.42), channel_id=1, replica_groups=mesh['y'=8,'z'=8,'core'=2,'x'=4] {'x'}, dimensions={0} | all-to-all | bytes 524288 | tf_op jit(solution)/shard_map/all_to_all | solution.py:213
  45.6 0.9 shard_map.43
  46.5 4.2 %all_to_all.53 = f32[2,8,72,128]{3,2,1,0:T(8,128)S(1)} all-to-all(f32[2,8,72,128]{3,2,1,0:T(8,128)S(1)} %shard_map.43), channel_id=1, replica_groups=mesh['y'=8,'z'=8,'core'=2,'x'=4] {'core'}, dimensions={0} | all-to-all | bytes 1179648 | tf_op jit(solution)/shard_map/all_to_all | solution.py:220
  50.7 15.5 %all_to_all.54 = f32[8,72,128]{2,1,0:T(8,128)S(1)} all-to-all(f32[8,72,128]{2,1,0:T(8,128)S(1)} %reduce_sum.27), channel_id=1, replica_groups=mesh['y'=8,'z'=8,'core'=2,'x'=4] {'y'}, dimensions={0} | all-to-all | bytes 589824 | tf_op jit(solution)/shard_map/all_to_all | solution.py:221
  66.3 15.0 %all_to_all.55.sums_ref = f32[8,72,128]{2,1,0:T(8,128)S(1)} all-to-all(f32[8,72,128]{2,1,0:T(8,128)S(1)} %broadcast_in_dim.7), channel_id=1, replica_groups=mesh['y'=8,'z'=8,'core'=2,'x'=4] {'z'}, dimensions={0} | all-to-all | bytes 589824 | tf_op jit(solution)/shard_map/all_to_all | solution.py:222
  81.3 0.0 copy-start.1
  81.3 1.1 shard_map.44
  82.4 13.2 %all_to_all.56.panel_ref = bf16[16,32,256]{2,1,0:T(8,128)(2,1)S(1)} all-to-all(bf16[16,32,256]{2,1,0:T(8,128)(2,1)S(1)} %shard_map.44), channel_id=1, replica_groups=mesh['y'=8,'z'=8,'core'=2,'x'=4] {'core','y'}, dimensions={0} | all-to-all | bytes 524288 | tf_op jit(solution)/shard_map/all_to_all | solution.py:230
  95.6 0.0 copy-done.1
  95.6 1.4 shard_map.45
  97.0 9.1 %all_to_all.57.parts_ref = f32[4,32,512]{2,1,0:T(8,128)S(1)} all-to-all(f32[4,32,512]{2,1,0:T(8,128)S(1)} %shard_map.45), channel_id=1, replica_groups=mesh['y'=8,'z'=8,'core'=2,'x'=4] {'x'}, dimensions={0} | all-to-all | bytes 524288 | tf_op jit(solution)/shard_map/all_to_all | solution.py:239
  106.0 1.1 shard_map.46
  107.1 4.6 %all_to_all.58 = f32[2,64,16,128]{3,2,1,0:T(8,128)S(1)} all-to-all(f32[2,64,16,128]{3,2,1,0:T(8,128)S(1)} %get-tuple-element.6), channel_id=1, replica_groups=mesh['y'=8,'z'=8,'core'=2,'x'=4] {'core'}, dimensions={0} | all-to-all | bytes 2097152 | tf_op jit(solution)/shard_map/all_to_all | solution.py:249
  111.6 0.1 reduce_sum.29
  111.8 24.5 %all_to_all.59.sums_ref = f32[64,16,128]{2,1,0:T(8,128)S(1)} all-to-all(f32[64,16,128]{2,1,0:T(8,128)S(1)} %reduce_sum.29), channel_id=1, replica_groups=mesh['y'=8,'z'=8,'core'=2,'x'=4] {'y','z'}, dimensions={0} | all-to-all | bytes 1048576 | tf_op jit(solution)/shard_map/all_to_all | solution.py:250
  136.2 1.8 %shard_map.47 = (f32[32,512]{1,0:T(8,128)}, f32[32,32]{1,0:T(8,128)}) custom-call(f32[64,16,128]{2,1,0:T(8,128)S(1)} %all_to_all.59.sums_ref, f32[32,512]{1,0:T(8,128)S(1)} %get-tuple-element.7.sketch_ref), custom_call_target="tpu_custom_call" | custom-call | flops 1048576 | bytes 1048576 | tf_op jit(solution)/shard_map/pallas_call | solution.py:23
  (4 shorter events, 0.1 us)
Async XLA Ops:
  0.6 0.7 copy-start.2
  1.3 33.4 %copy-start = (bf16[512,4096]{1,0:T(8,128)(2,1)S(1)}, bf16[512,4096]{1,0:T(8,128)(2,1)}, u32[]{:S(2)}) copy-start(bf16[512,4096]{1,0:T(8,128)(2,1)} %transport_ref.7) | copy-start | bytes 12582916
  81.3 14.3 %copy-start.1 = (bf16[512,4096]{1,0:T(8,128)(2,1)S(1)}, bf16[512,4096]{1,0:T(8,128)(2,1)}, u32[]{:S(2)}) copy-start(bf16[512,4096]{1,0:T(8,128)(2,1)} %transport_ref.7) | copy-start | bytes 12582916

commit v6 on v5

--- a/solution.py
+++ b/solution.py
@@ -168,12 +168,37 @@
             out_ref[core, chip, 8:16] = gram
 
 
-def normalise(total_rows, sums_ref, out_ref):
-    peers, height, _ = sums_ref.shape
-    total = sums_ref[0]
-    for p in range(1, peers):
-        total = total + sums_ref[p]
-    tiles = height // 8 - 1
+def encode(total):
+    gram = total[-8:]
+    terms = []
+    for _ in range(3):
+        terms.append(gram.astype(BF16).astype(F32))
+        gram = gram - terms[-1]
+    return jnp.concatenate([total[:-8]] + terms).astype(BF16)
+
+
+def decoded_sum(messages_ref):
+    total = messages_ref[0].astype(F32)
+    for p in range(1, messages_ref.shape[0]):
+        total = total + messages_ref[p].astype(F32)
+    gram = (total[-8:] + total[-16:-8]) + total[-24:-16]
+    return jnp.concatenate([total[:-24], gram])
+
+
+def add_cores(sums_ref, out_ref):
+    for peer in range(out_ref.shape[0]):
+        out_ref[peer] = encode(sums_ref[0, peer] + sums_ref[1, peer])
+
+
+def add_peers(messages_ref, out_ref):
+    message = encode(decoded_sum(messages_ref))
+    for copy in range(out_ref.shape[0]):
+        out_ref[copy] = message
+
+
+def normalise(total_rows, messages_ref, out_ref):
+    total = decoded_sum(messages_ref)
+    tiles = total.shape[0] // 8 - 1
     inverse = inverse_factor(unpack_square(total[8 * tiles :]) / total_rows)
     for c in range(tiles // 4):
         block = total[32 * c : 32 * c + 32]
@@ -217,9 +242,11 @@
     sums = kernel_call(
         middle_product, shape((2, ny, height, 128), F32), flops, 5 << 20, parts, transport
     )
-    sums = jnp.sum(lax.all_to_all(sums, "core", 0, 0), axis=0)
-    sums = jnp.sum(lax.all_to_all(sums, "y", 0, 0), axis=0)
-    sums = lax.all_to_all(jnp.broadcast_to(sums, (nz, height, 128)), "z", 0, 0)
+    sums = lax.all_to_all(sums, "core", 0, 0)
+    sums = kernel_call(add_cores, shape((ny, height + 16, 128), BF16), 0, 1 << 20, sums)
+    sums = lax.all_to_all(sums, "y", 0, 0)
+    sums = kernel_call(add_peers, shape((nz, height + 16, 128), BF16), 0, 1 << 20, sums)
+    sums = lax.all_to_all(sums, "z", 0, 0)
     panel = kernel_call(
         functools.partial(normalise, total_rows),
         shape((2 * ny, RANK, width), BF16),

time: 140 us -> 135 us (0.964)
  blocking collectives: 129 us -> 123 us
    all_to_all x2 -> x1, blocking collectives: 8.78 us -> 4.57 us  [on_device(): sums = jnp.sum(lax.all_to_all(sums, 'core', 0, 0), axis=0)]
    all_to_all x2 -> x3, blocking collectives: 30.6 us -> 29.3 us  [the longest x1 13.1 us: on_device(): sums = lax.all_to_all(sums, 'y', 0, 0)]
    pallas_call x7 -> x9, Pallas kernels: 7.51 us -> 7.59 us  [kernel_call(): pl.pallas_call(body, out_shape=outs, in_specs=[VMEM] * len(args), out_spe...]
where the time goes in v6:
time: 135 us; the launch traced here: 132 us
  blocking collectives  123 us (91%)
  Pallas kernels  7.59 us (6%)
    all_to_all x1, blocking collectives, on_device(): tiles = lax.all_to_all(copies, CHIPS, 0, 0)  29.4 us
    all_to_all x1, blocking collectives, on_device(): sums = lax.all_to_all(sums, CHIPS, 0, 0)  24.6 us
    all_to_all x2, blocking collectives, on_device(): parts = lax.all_to_all(partial, 'x', 0, 0)  18.5 us
    all_to_all x1, blocking collectives, on_device(): sums = lax.all_to_all(sums, 'y', 0, 0)  13.1 us
    all_to_all x1, blocking collectives, on_device(): panel = lax.all_to_all(panel, ('core', 'y'), 0, 0)  13.1 us
    all_to_all x1, blocking collectives, on_device(): sums = lax.all_to_all(sums, 'z', 0, 0)  12 us
    pallas_call x9, Pallas kernels, kernel_call(): pl.pallas_call(body, out_shape=outs, in_specs=[VMEM] * len(args), out_spe...  7.59 us
    all_to_all x1, blocking collectives, on_device(): sums = jnp.sum(lax.all_to_all(sums, 'core', 0, 0), axis=0)  4.57 us

profile of v6, /device:TPU:6, one launch (start us, length us, event | category | flops | bytes accessed | tf_op | source)
XLA Modules:
  0.0 132.5 jit_solution(2544815704236895329)
XLA Ops:
  0.6 0.0 copy-start.1
  0.6 0.7 copy-done.1
  1.3 0.0 copy-start
  1.3 0.1 shard_map.41
  1.4 29.4 %all_to_all.50 = bf16[64,8,128]{2,1,0:T(8,128)(2,1)S(1)} all-to-all(bf16[64,8,128]{2,1,0:T(8,128)(2,1)S(1)} %shard_map.41), channel_id=1, replica_groups=mesh['y'=8,'z'=8,'core'=2,'x'=4] {'y','z'}, dimensions={0} | all-to-all | bytes 262144 | tf_op jit(solution)/shard_map/all_to_all | solution.py:233
  30.8 3.9 %all_to_all.51.tiles_ref = bf16[2,64,8,128]{3,2,1,0:T(8,128)(2,1)S(1)} all-to-all(bf16[2,64,8,128]{3,2,1,0:T(8,128)(2,1)S(1)} %broadcast_in_dim.3), channel_id=1, replica_groups=mesh['y'=8,'z'=8,'core'=2,'x'=4] {'core'}, dimensions={0} | all-to-all | bytes 524288 | tf_op jit(solution)/shard_map/all_to_all | solution.py:234
  34.7 0.0 copy-done
  34.7 1.3 shard_map.42
  36.1 9.5 %all_to_all.52.parts_ref = f32[4,32,512]{2,1,0:T(8,128)S(1)} all-to-all(f32[4,32,512]{2,1,0:T(8,128)S(1)} %shard_map.42), channel_id=1, replica_groups=mesh['y'=8,'z'=8,'core'=2,'x'=4] {'x'}, dimensions={0} | all-to-all | bytes 524288 | tf_op jit(solution)/shard_map/all_to_all | solution.py:238
  45.6 0.9 shard_map.43
  46.5 4.2 %all_to_all.53.sums_ref = f32[2,8,72,128]{3,2,1,0:T(8,128)S(1)} all-to-all(f32[2,8,72,128]{3,2,1,0:T(8,128)S(1)} %shard_map.43), channel_id=1, replica_groups=mesh['y'=8,'z'=8,'core'=2,'x'=4] {'core'}, dimensions={0} | all-to-all | bytes 1179648 | tf_op jit(solution)/shard_map/all_to_all | solution.py:245
  50.7 13.1 %all_to_all.54.messages_ref = bf16[8,88,128]{2,1,0:T(8,128)(2,1)S(1)} all-to-all(bf16[8,88,128]{2,1,0:T(8,128)(2,1)S(1)} %shard_map.44), channel_id=1, replica_groups=mesh['y'=8,'z'=8,'core'=2,'x'=4] {'y'}, dimensions={0} | all-to-all | bytes 360448 | tf_op jit(solution)/shard_map/all_to_all | solution.py:247
  63.8 12.0 %all_to_all.55.messages_ref = bf16[8,88,128]{2,1,0:T(8,128)(2,1)S(1)} all-to-all(bf16[8,88,128]{2,1,0:T(8,128)(2,1)S(1)} %shard_map.45), channel_id=1, replica_groups=mesh['y'=8,'z'=8,'core'=2,'x'=4] {'z'}, dimensions={0} | all-to-all | bytes 360448 | tf_op jit(solution)/shard_map/all_to_all | solution.py:249
  75.8 1.1 shard_map.46
  76.9 13.1 %all_to_all.56.panel_ref = bf16[16,32,256]{2,1,0:T(8,128)(2,1)S(1)} all-to-all(bf16[16,32,256]{2,1,0:T(8,128)(2,1)S(1)} %shard_map.46), channel_id=1, replica_groups=mesh['y'=8,'z'=8,'core'=2,'x'=4] {'core','y'}, dimensions={0} | all-to-all | bytes 524288 | tf_op jit(solution)/shard_map/all_to_all | solution.py:257
  90.0 1.4 %shard_map.47 = f32[4,32,512]{2,1,0:T(8,128)S(1)} custom-call(bf16[16,32,256]{2,1,0:T(8,128)(2,1)S(1)} %all_to_all.56.panel_ref, bf16[512,4096]{1,0:T(8,128)(2,1)S(1)} %copy-done), custom_call_target="tpu_custom_call" | custom-call | flops 536870912 | bytes 5242880 | tf_op jit(solution)/shard_map/pallas_call | solution.py:23
  91.3 9.1 %all_to_all.57.parts_ref = f32[4,32,512]{2,1,0:T(8,128)S(1)} all-to-all(f32[4,32,512]{2,1,0:T(8,128)S(1)} %shard_map.47), channel_id=1, replica_groups=mesh['y'=8,'z'=8,'core'=2,'x'=4] {'x'}, dimensions={0} | all-to-all | bytes 524288 | tf_op jit(solution)/shard_map/all_to_all | solution.py:266
  100.4 1.1 shard_map.48
  101.5 4.6 %all_to_all.58 = f32[2,64,16,128]{3,2,1,0:T(8,128)S(1)} all-to-all(f32[2,64,16,128]{3,2,1,0:T(8,128)S(1)} %get-tuple-element.6), channel_id=1, replica_groups=mesh['y'=8,'z'=8,'core'=2,'x'=4] {'core'}, dimensions={0} | all-to-all | bytes 2097152 | tf_op jit(solution)/shard_map/all_to_all | solution.py:276
  106.0 0.1 reduce_sum.9
  106.1 24.6 %all_to_all.59.sums_ref = f32[64,16,128]{2,1,0:T(8,128)S(1)} all-to-all(f32[64,16,128]{2,1,0:T(8,128)S(1)} %reduce_sum.9), channel_id=1, replica_groups=mesh['y'=8,'z'=8,'core'=2,'x'=4] {'y','z'}, dimensions={0} | all-to-all | bytes 1048576 | tf_op jit(solution)/shard_map/all_to_all | solution.py:277
  130.7 1.8 %shard_map.49 = (f32[32,512]{1,0:T(8,128)}, f32[32,32]{1,0:T(8,128)}) custom-call(f32[64,16,128]{2,1,0:T(8,128)S(1)} %all_to_all.59.sums_ref, f32[32,512]{1,0:T(8,128)S(1)} %get-tuple-element.7.sketch_ref), custom_call_target="tpu_custom_call" | custom-call | flops 1048576 | bytes 1048576 | tf_op jit(solution)/shard_map/pallas_call | solution.py:23
  (3 shorter events, 0.1 us)
Async XLA Ops:
  0.6 0.7 copy-start.1
  1.3 33.4 %copy-start = (bf16[512,4096]{1,0:T(8,128)(2,1)S(1)}, bf16[512,4096]{1,0:T(8,128)(2,1)}, u32[]{:S(2)}) copy-start(bf16[512,4096]{1,0:T(8,128)(2,1)} %transport_ref.7) | copy-start | bytes 12582916

commit v7 on v6

--- a/solution.py
+++ b/solution.py
@@ -45,6 +45,24 @@
 
 def unpack_square(tile):
     return jnp.concatenate([tile] + [pltpu.roll(tile, 128 - 32 * q, axis=1) for q in range(1, 4)])
+
+
+def pack_lower(square):
+    lane = lanes_of((8, 128))
+    out = jnp.where(lane < 32, square[24:32], 0.0)
+    for at, width, first in ((32, 24, 16), (56, 16, 8), (72, 8, 0)):
+        block = pltpu.roll(square[first : first + 8], at, axis=1)
+        out = jnp.where((lane >= at) & (lane < at + width), block, out)
+    return out
+
+
+def unpack_lower(tile):
+    lower = jnp.concatenate([pltpu.roll(tile, 128 - at, axis=1) for at in (72, 56, 32)] + [tile])
+    lane = lanes_of((RANK, 128))
+    row = lax.broadcasted_iota(jnp.int32, (RANK, 128), 0)
+    lower = jnp.where(lane <= row, lower, 0.0)
+    turned = jnp.concatenate([lower, jnp.zeros((128 - RANK, 128), F32)]).T[:RANK]
+    return jnp.where(lane <= row, lower, turned)
 
 
 def inverse_factor(gram):
@@ -126,7 +144,7 @@
         out = jnp.dot(both, transport_ref[:, at : at + width], preferred_element_type=F32)
         return out[:RANK] + out[RANK:]
 
-    return sketch, pack_square(gram), columns
+    return sketch, pack_lower(gram), columns
 
 
 def middle_product(parts_ref, transport_ref, out_ref):
@@ -169,20 +187,27 @@
 
 
 def encode(total):
+    lane = lanes_of((8, 128))
     gram = total[-8:]
     terms = []
     for _ in range(3):
         terms.append(gram.astype(BF16).astype(F32))
         gram = gram - terms[-1]
-    return jnp.concatenate([total[:-8]] + terms).astype(BF16)
+    middle = pltpu.roll(terms[1], 80, axis=1)
+    first = jnp.where(lane < 80, terms[0], middle)
+    second = jnp.where(lane < 32, middle, pltpu.roll(terms[2], 32, axis=1))
+    return jnp.concatenate([total[:-8], first, second]).astype(BF16)
 
 
 def decoded_sum(messages_ref):
     total = messages_ref[0].astype(F32)
     for p in range(1, messages_ref.shape[0]):
         total = total + messages_ref[p].astype(F32)
-    gram = (total[-8:] + total[-16:-8]) + total[-24:-16]
-    return jnp.concatenate([total[:-24], gram])
+    lane = lanes_of((8, 128))
+    first, second = total[-16:-8], total[-8:]
+    middle = pltpu.roll(jnp.where(lane < 32, second, first), 48, axis=1)
+    gram = (pltpu.roll(second, 96, axis=1) + middle) + first
+    return jnp.concatenate([total[:-16], jnp.where(lane < 80, gram, 0.0)])
 
 
 def add_cores(sums_ref, out_ref):
@@ -199,7 +224,7 @@
 def normalise(total_rows, messages_ref, out_ref):
     total = decoded_sum(messages_ref)
     tiles = total.shape[0] // 8 - 1
-    inverse = inverse_factor(unpack_square(total[8 * tiles :]) / total_rows)
+    inverse = inverse_factor(unpack_lower(total[8 * tiles :]) / total_rows)
     for c in range(tiles // 4):
         block = total[32 * c : 32 * c + 32]
         panel = jnp.dot(inverse, block, precision=HIGHEST, preferred_element_type=F32).astype(BF16)
@@ -207,11 +232,9 @@
             out_ref[copy, :, 128 * c : 128 * c + 128] = panel
 
 
-def finish(total_rows, sums_ref, sketch_ref, basis_ref, coimage_ref):
-    total = sums_ref[0]
-    for p in range(1, sums_ref.shape[0]):
-        total = total + sums_ref[p]
-    inverse = inverse_factor(unpack_square(total[8:16]) / total_rows)
+def finish(total_rows, messages_ref, sketch_ref, basis_ref, coimage_ref):
+    total = decoded_sum(messages_ref)
+    inverse = inverse_factor(unpack_lower(total[8:]) / total_rows)
     basis_ref[...] = jnp.dot(
         inverse, sketch_ref[...], precision=HIGHEST, preferred_element_type=F32
     )
@@ -243,9 +266,9 @@
         middle_product, shape((2, ny, height, 128), F32), flops, 5 << 20, parts, transport
     )
     sums = lax.all_to_all(sums, "core", 0, 0)
-    sums = kernel_call(add_cores, shape((ny, height + 16, 128), BF16), 0, 1 << 20, sums)
+    sums = kernel_call(add_cores, shape((ny, height + 8, 128), BF16), 0, 1 << 20, sums)
     sums = lax.all_to_all(sums, "y", 0, 0)
-    sums = kernel_call(add_peers, shape((nz, height + 16, 128), BF16), 0, 1 << 20, sums)
+    sums = kernel_call(add_peers, shape((nz, height + 8, 128), BF16), 0, 1 << 20, sums)
     sums = lax.all_to_all(sums, "z", 0, 0)
     panel = kernel_call(
         functools.partial(normalise, total_rows),
@@ -273,7 +296,8 @@
         parts,
         transport,
     )
-    sums = jnp.sum(lax.all_to_all(sums, "core", 0, 0), axis=0)
+    sums = lax.all_to_all(sums, "core", 0, 0)
+    sums = kernel_call(add_cores, shape((chips, 24, 128), BF16), 0, 1 << 20, sums)
     sums = lax.all_to_all(sums, CHIPS, 0, 0)
     basis, coimage = kernel_call(
         functools.partial(finish, total_rows),

time: 135 us -> 132 us (0.978)
  blocking collectives: 123 us -> 121 us
    all_to_all x1 -> x0, blocking collectives: 4.57 us -> none  [on_device(): sums = jnp.sum(lax.all_to_all(sums, 'core', 0, 0), axis=0)]
    all_to_all x1 -> x2, blocking collectives: 4.21 us -> 8.78 us  [on_device(): sums = lax.all_to_all(sums, 'core', 0, 0)]
    all_to_all x1, blocking collectives: 24.6 us -> 22.4 us  [on_device(): sums = lax.all_to_all(sums, CHIPS, 0, 0)]
    pallas_call x9 -> x10, Pallas kernels: 7.59 us -> 8.32 us  [kernel_call(): pl.pallas_call(body, out_shape=outs, in_specs=[VMEM] * len(args), out_spe...]
where the time goes in v7:
time: 132 us; the launch traced here: 130 us
  blocking collectives  121 us (92%)
  Pallas kernels  8.32 us (6%)
    all_to_all x1, blocking collectives, on_device(): tiles = lax.all_to_all(copies, CHIPS, 0, 0)  29.4 us
    all_to_all x1, blocking collectives, on_device(): sums = lax.all_to_all(sums, CHIPS, 0, 0)  22.4 us
    all_to_all x2, blocking collectives, on_device(): parts = lax.all_to_all(partial, 'x', 0, 0)  18.5 us
    all_to_all x1, blocking collectives, on_device(): panel = lax.all_to_all(panel, ('core', 'y'), 0, 0)  13.1 us
    all_to_all x1, blocking collectives, on_device(): sums = lax.all_to_all(sums, 'y', 0, 0)  12.7 us
    all_to_all x1, blocking collectives, on_device(): sums = lax.all_to_all(sums, 'z', 0, 0)  11.8 us
    all_to_all x2, blocking collectives, on_device(): sums = lax.all_to_all(sums, 'core', 0, 0)  8.78 us
    pallas_call x10, Pallas kernels, kernel_call(): pl.pallas_call(body, out_shape=outs, in_specs=[VMEM] * len(args), out_spe...  8.32 us

profile of v7, /device:TPU:6, one launch (start us, length us, event | category | flops | bytes accessed | tf_op | source)
XLA Modules:
  0.0 130.4 jit_solution(6423686645518732150)
XLA Ops:
  0.6 0.0 copy-start.1
  0.6 0.7 copy-done.1
  1.3 0.0 copy-start
  1.3 0.1 shard_map.41
  1.4 29.4 %all_to_all.50 = bf16[64,8,128]{2,1,0:T(8,128)(2,1)S(1)} all-to-all(bf16[64,8,128]{2,1,0:T(8,128)(2,1)S(1)} %shard_map.41), channel_id=1, replica_groups=mesh['y'=8,'z'=8,'core'=2,'x'=4] {'y','z'}, dimensions={0} | all-to-all | bytes 262144 | tf_op jit(solution)/shard_map/all_to_all | solution.py:256
  30.8 3.9 %all_to_all.51.tiles_ref = bf16[2,64,8,128]{3,2,1,0:T(8,128)(2,1)S(1)} all-to-all(bf16[2,64,8,128]{3,2,1,0:T(8,128)(2,1)S(1)} %broadcast_in_dim.3), channel_id=1, replica_groups=mesh['y'=8,'z'=8,'core'=2,'x'=4] {'core'}, dimensions={0} | all-to-all | bytes 524288 | tf_op jit(solution)/shard_map/all_to_all | solution.py:257
  34.7 0.0 copy-done
  34.7 1.3 %shard_map.42 = f32[4,32,512]{2,1,0:T(8,128)S(1)} custom-call(bf16[2,64,8,128]{3,2,1,0:T(8,128)(2,1)S(1)} %all_to_all.51.tiles_ref, bf16[512,4096]{1,0:T(8,128)(2,1)S(1)} %copy-done), custom_call_target="tpu_custom_call" | custom-call | flops 536870912 | bytes 5242880 | tf_op jit(solution)/shard_map/pallas_call | solution.py:23
  36.1 9.5 %all_to_all.52.parts_ref = f32[4,32,512]{2,1,0:T(8,128)S(1)} all-to-all(f32[4,32,512]{2,1,0:T(8,128)S(1)} %shard_map.42), channel_id=1, replica_groups=mesh['y'=8,'z'=8,'core'=2,'x'=4] {'x'}, dimensions={0} | all-to-all | bytes 524288 | tf_op jit(solution)/shard_map/all_to_all | solution.py:261
  45.6 0.9 shard_map.43
  46.5 4.2 %all_to_all.53.sums_ref = f32[2,8,72,128]{3,2,1,0:T(8,128)S(1)} all-to-all(f32[2,8,72,128]{3,2,1,0:T(8,128)S(1)} %shard_map.43), channel_id=1, replica_groups=mesh['y'=8,'z'=8,'core'=2,'x'=4] {'core'}, dimensions={0} | all-to-all | bytes 1179648 | tf_op jit(solution)/shard_map/all_to_all | solution.py:268
  50.7 0.1 shard_map.44
  50.8 12.7 %all_to_all.54.messages_ref = bf16[8,80,128]{2,1,0:T(8,128)(2,1)S(1)} all-to-all(bf16[8,80,128]{2,1,0:T(8,128)(2,1)S(1)} %shard_map.44), channel_id=1, replica_groups=mesh['y'=8,'z'=8,'core'=2,'x'=4] {'y'}, dimensions={0} | all-to-all | bytes 327680 | tf_op jit(solution)/shard_map/all_to_all | solution.py:270
  63.5 0.2 shard_map.45
  63.7 11.8 %all_to_all.55.messages_ref = bf16[8,80,128]{2,1,0:T(8,128)(2,1)S(1)} all-to-all(bf16[8,80,128]{2,1,0:T(8,128)(2,1)S(1)} %shard_map.45), channel_id=1, replica_groups=mesh['y'=8,'z'=8,'core'=2,'x'=4] {'z'}, dimensions={0} | all-to-all | bytes 327680 | tf_op jit(solution)/shard_map/all_to_all | solution.py:272
  75.5 1.3 shard_map.46
  76.7 13.1 %all_to_all.56.panel_ref = bf16[16,32,256]{2,1,0:T(8,128)(2,1)S(1)} all-to-all(bf16[16,32,256]{2,1,0:T(8,128)(2,1)S(1)} %shard_map.46), channel_id=1, replica_groups=mesh['y'=8,'z'=8,'core'=2,'x'=4] {'core','y'}, dimensions={0} | all-to-all | bytes 524288 | tf_op jit(solution)/shard_map/all_to_all | solution.py:280
  89.8 1.4 %shard_map.47 = f32[4,32,512]{2,1,0:T(8,128)S(1)} custom-call(bf16[16,32,256]{2,1,0:T(8,128)(2,1)S(1)} %all_to_all.56.panel_ref, bf16[512,4096]{1,0:T(8,128)(2,1)S(1)} %copy-done), custom_call_target="tpu_custom_call" | custom-call | flops 536870912 | bytes 5242880 | tf_op jit(solution)/shard_map/pallas_call | solution.py:23
  91.2 9.1 %all_to_all.57.parts_ref = f32[4,32,512]{2,1,0:T(8,128)S(1)} all-to-all(f32[4,32,512]{2,1,0:T(8,128)S(1)} %shard_map.47), channel_id=1, replica_groups=mesh['y'=8,'z'=8,'core'=2,'x'=4] {'x'}, dimensions={0} | all-to-all | bytes 524288 | tf_op jit(solution)/shard_map/all_to_all | solution.py:289
  100.2 1.1 shard_map.48
  101.3 4.6 %all_to_all.58.sums_ref = f32[2,64,16,128]{3,2,1,0:T(8,128)S(1)} all-to-all(f32[2,64,16,128]{3,2,1,0:T(8,128)S(1)} %get-tuple-element.6), channel_id=1, replica_groups=mesh['y'=8,'z'=8,'core'=2,'x'=4] {'core'}, dimensions={0} | all-to-all | bytes 2097152 | tf_op jit(solution)/shard_map/all_to_all | solution.py:299
  105.9 0.2 shard_map.49
  106.0 22.4 %all_to_all.59.messages_ref = bf16[64,24,128]{2,1,0:T(8,128)(2,1)S(1)} all-to-all(bf16[64,24,128]{2,1,0:T(8,128)(2,1)S(1)} %shard_map.49), channel_id=1, replica_groups=mesh['y'=8,'z'=8,'core'=2,'x'=4] {'y','z'}, dimensions={0} | all-to-all | bytes 786432 | tf_op jit(solution)/shard_map/all_to_all | solution.py:301
  128.4 2.0 %shard_map.50 = (f32[32,512]{1,0:T(8,128)}, f32[32,32]{1,0:T(8,128)}) custom-call(bf16[64,24,128]{2,1,0:T(8,128)(2,1)S(1)} %all_to_all.59.messages_ref, f32[32,512]{1,0:T(8,128)S(1)} %get-tuple-element.7.sketch_ref), custom_call_target="tpu_custom_call" | custom-call | flops 1048576 | bytes 1048576 | tf_op jit(solution)/shard_map/pallas_call | solution.py:23
  (1 shorter events, 0.0 us)
Async XLA Ops:
  0.6 0.7 copy-start.1
  1.3 33.4 %copy-start = (bf16[512,4096]{1,0:T(8,128)(2,1)S(1)}, bf16[512,4096]{1,0:T(8,128)(2,1)}, u32[]{:S(2)}) copy-start(bf16[512,4096]{1,0:T(8,128)(2,1)} %transport_ref.7) | copy-start | bytes 12582916

commit v8 on v7

--- a/solution.py
+++ b/solution.py
@@ -70,7 +70,7 @@
     row = lax.broadcasted_iota(jnp.int32, (RANK, 128), 0)
     work = jnp.where(lane < RANK, gram, jnp.where(lane == row + RANK, 1.0, 0.0))
     pivots = jnp.ones((RANK, 128), F32)
-    width = 8
+    width = 16
     for start in range(0, RANK, width):
         columns = [
             jnp.broadcast_to(work[:, start + i : start + i + 1], (RANK, 128)) for i in range(width)
@@ -147,22 +147,25 @@
     return sketch, pack_lower(gram), columns
 
 
-def middle_product(parts_ref, transport_ref, out_ref):
-    cores, groups, height, _ = out_ref.shape
-    tiles = height // 8 - 1
-    width = tiles // 4 * 128
+def middle_product(groups, parts_ref, transport_ref, out_ref):
+    cores, height, _ = out_ref.shape
+    cols = transport_ref.shape[1]
+    width = cols // (cores * groups)
     _, gram, columns = product(parts_ref, transport_ref)
+    for group in range(groups):
+        for core in range(cores):
+            block = columns((group * cores + core) * width, width)
+            for t in range(width // 32):
+                a, c = t % 4, t // 4
+                at = group * width // 4 + 8 * t
+                out_ref[core, at : at + 8] = block[8 * a : 8 * a + 8, 128 * c : 128 * c + 128]
     for core in range(cores):
-        for g in range(groups):
-            block = columns((core * groups + g) * width, width)
-            for t in range(tiles):
-                a, c = t % 4, t // 4
-                out_ref[core, g, 8 * t : 8 * t + 8] = block[8 * a : 8 * a + 8, 128 * c : 128 * c + 128]
-            out_ref[core, g, 8 * tiles : height] = gram
+        out_ref[core, height - 8 : height] = gram
 
 
 def last_product(parts_ref, transport_ref, out_ref, sketch_ref):
-    cores, chips, _, _ = out_ref.shape
+    cores, height, _ = out_ref.shape
+    chips = height // 8 - 1
     sketch, gram, columns = product(parts_ref, transport_ref)
     sketch_ref[...] = sketch
     lane = lanes_of((8, 128))
@@ -180,15 +183,15 @@
                 v1 = jnp.where(even, pltpu.roll(u[a], 96, axis=1), u[a + 1])
                 for b, v in ((a, v0), (a + 1, v1)):
                     device = 16 * wide + 4 * c + b
-                    out_ref[device % 2, device // 2, 0:8] = v
+                    y, z = divmod(device // 2, 8)
+                    at = 8 * (z * (chips // 8) + y)
+                    out_ref[device % 2, at : at + 8] = v
     for core in range(cores):
-        for chip in range(chips):
-            out_ref[core, chip, 8:16] = gram
-
-
-def encode(total):
-    lane = lanes_of((8, 128))
-    gram = total[-8:]
+        out_ref[core, height - 8 : height] = gram
+
+
+def three_terms(gram):
+    lane = lanes_of((8, 128))
     terms = []
     for _ in range(3):
         terms.append(gram.astype(BF16).astype(F32))
@@ -196,7 +199,7 @@
     middle = pltpu.roll(terms[1], 80, axis=1)
     first = jnp.where(lane < 80, terms[0], middle)
     second = jnp.where(lane < 32, middle, pltpu.roll(terms[2], 32, axis=1))
-    return jnp.concatenate([total[:-8], first, second]).astype(BF16)
+    return jnp.concatenate([first, second])
 
 
 def decoded_sum(messages_ref):
@@ -211,12 +214,18 @@
 
 
 def add_cores(sums_ref, out_ref):
-    for peer in range(out_ref.shape[0]):
-        out_ref[peer] = encode(sums_ref[0, peer] + sums_ref[1, peer])
+    peers, height, _ = out_ref.shape
+    rows = height - 16
+    gram = three_terms(sums_ref[0, peers * rows :] + sums_ref[1, peers * rows :])
+    for peer in range(peers):
+        at = slice(peer * rows, (peer + 1) * rows)
+        block = sums_ref[0, at] + sums_ref[1, at]
+        out_ref[peer] = jnp.concatenate([block, gram]).astype(BF16)
 
 
 def add_peers(messages_ref, out_ref):
-    message = encode(decoded_sum(messages_ref))
+    total = decoded_sum(messages_ref)
+    message = jnp.concatenate([total[:-8], three_terms(total[-8:])]).astype(BF16)
     for copy in range(out_ref.shape[0]):
         out_ref[copy] = message
 
@@ -261,14 +270,14 @@
     parts = lax.all_to_all(partial, "x", 0, 0)
 
     width = cols // (2 * ny)
-    height = RANK * width // 128 + 8
+    height = RANK * width // 128
     sums = kernel_call(
-        middle_product, shape((2, ny, height, 128), F32), flops, 5 << 20, parts, transport
+        functools.partial(middle_product, ny), shape((2, ny * height + 8, 128), F32), flops, 5 << 20, parts, transport
     )
     sums = lax.all_to_all(sums, "core", 0, 0)
-    sums = kernel_call(add_cores, shape((ny, height + 8, 128), BF16), 0, 1 << 20, sums)
+    sums = kernel_call(add_cores, shape((ny, height + 16, 128), BF16), 0, 1 << 20, sums)
     sums = lax.all_to_all(sums, "y", 0, 0)
-    sums = kernel_call(add_peers, shape((nz, height + 8, 128), BF16), 0, 1 << 20, sums)
+    sums = kernel_call(add_peers, shape((nz, height + 16, 128), BF16), 0, 1 << 20, sums)
     sums = lax.all_to_all(sums, "z", 0, 0)
     panel = kernel_call(
         functools.partial(normalise, total_rows),
@@ -277,7 +286,7 @@
         8 << 20,
         sums,
     )
-    panel = lax.all_to_all(panel, ("core", "y"), 0, 0)
+    panel = lax.all_to_all(panel, ("y", "core"), 0, 0)
     partial = kernel_call(
         next_sketch,
         shape((nx, RANK, rows), F32),
@@ -290,7 +299,7 @@
 
     sums, sketch = kernel_call(
         last_product,
-        (shape((2, chips, 16, 128), F32), shape((RANK, rows), F32)),
+        (shape((2, 8 * chips + 8, 128), F32), shape((RANK, rows), F32)),
         flops,
         6 << 20,
         parts,
@@ -298,7 +307,7 @@
     )
     sums = lax.all_to_all(sums, "core", 0, 0)
     sums = kernel_call(add_cores, shape((chips, 24, 128), BF16), 0, 1 << 20, sums)
-    sums = lax.all_to_all(sums, CHIPS, 0, 0)
+    sums = lax.all_to_all(sums, ("z", "y"), 0, 0)
     basis, coimage = kernel_call(
         functools.partial(finish, total_rows),
         (shape((RANK, rows), F32), shape((RANK, RANK), F32)),

time: 132 us -> 132 us (level)
  no operation moved by 1% of the time
where the time goes in v8:
time: 132 us; the launch traced here: 130 us
  blocking collectives  121 us (92%)
  Pallas kernels  7.93 us (6%)
    all_to_all x1, blocking collectives, on_device(): tiles = lax.all_to_all(copies, CHIPS, 0, 0)  29.4 us
    all_to_all x1, blocking collectives, on_device(): sums = lax.all_to_all(sums, ('z', 'y'), 0, 0)  21.5 us
    all_to_all x2, blocking collectives, on_device(): parts = lax.all_to_all(partial, 'x', 0, 0)  19.8 us
    all_to_all x1, blocking collectives, on_device(): panel = lax.all_to_all(panel, ('y', 'core'), 0, 0)  13.6 us
    all_to_all x1, blocking collectives, on_device(): sums = lax.all_to_all(sums, 'y', 0, 0)  12.7 us
    all_to_all x1, blocking collectives, on_device(): sums = lax.all_to_all(sums, 'z', 0, 0)  11.8 us
    all_to_all x2, blocking collectives, on_device(): sums = lax.all_to_all(sums, 'core', 0, 0)  8.26 us
    pallas_call x10, Pallas kernels, kernel_call(): pl.pallas_call(body, out_shape=outs, in_specs=[VMEM] * len(args), out_spe...  7.93 us

profile of v8, /device:TPU:6, one launch (start us, length us, event | category | flops | bytes accessed | tf_op | source)
XLA Modules:
  0.0 130.3 jit_solution(13300037160485111583)
XLA Ops:
  0.6 0.0 copy-start.1
  0.6 0.7 copy-done.1
  1.3 0.0 copy-start
  1.3 0.1 shard_map.41
  1.4 29.4 %all_to_all.50 = bf16[64,8,128]{2,1,0:T(8,128)(2,1)S(1)} all-to-all(bf16[64,8,128]{2,1,0:T(8,128)(2,1)S(1)} %shard_map.41), channel_id=1, replica_groups=mesh['y'=8,'z'=8,'core'=2,'x'=4] {'y','z'}, dimensions={0} | all-to-all | bytes 262144 | tf_op jit(solution)/shard_map/all_to_all | solution.py:265
  30.8 3.9 %all_to_all.51.tiles_ref = bf16[2,64,8,128]{3,2,1,0:T(8,128)(2,1)S(1)} all-to-all(bf16[2,64,8,128]{3,2,1,0:T(8,128)(2,1)S(1)} %broadcast_in_dim.3), channel_id=1, replica_groups=mesh['y'=8,'z'=8,'core'=2,'x'=4] {'core'}, dimensions={0} | all-to-all | bytes 524288 | tf_op jit(solution)/shard_map/all_to_all | solution.py:266
  34.7 0.0 copy-done
  34.7 1.3 %shard_map.42 = f32[4,32,512]{2,1,0:T(8,128)S(1)} custom-call(bf16[2,64,8,128]{3,2,1,0:T(8,128)(2,1)S(1)} %all_to_all.51.tiles_ref, bf16[512,4096]{1,0:T(8,128)(2,1)S(1)} %copy-done), custom_call_target="tpu_custom_call" | custom-call | flops 536870912 | bytes 5242880 | tf_op jit(solution)/shard_map/pallas_call | solution.py:23
  36.1 9.5 %all_to_all.52.parts_ref = f32[4,32,512]{2,1,0:T(8,128)S(1)} all-to-all(f32[4,32,512]{2,1,0:T(8,128)S(1)} %shard_map.42), channel_id=1, replica_groups=mesh['y'=8,'z'=8,'core'=2,'x'=4] {'x'}, dimensions={0} | all-to-all | bytes 524288 | tf_op jit(solution)/shard_map/all_to_all | solution.py:270
  45.6 0.9 shard_map.43
  46.5 4.1 %all_to_all.53.sums_ref = f32[2,520,128]{2,1,0:T(8,128)S(1)} all-to-all(f32[2,520,128]{2,1,0:T(8,128)S(1)} %shard_map.43), channel_id=1, replica_groups=mesh['y'=8,'z'=8,'core'=2,'x'=4] {'core'}, dimensions={0} | all-to-all | bytes 1064960 | tf_op jit(solution)/shard_map/all_to_all | solution.py:277
  50.6 0.1 shard_map.44
  50.7 12.7 %all_to_all.54.messages_ref = bf16[8,80,128]{2,1,0:T(8,128)(2,1)S(1)} all-to-all(bf16[8,80,128]{2,1,0:T(8,128)(2,1)S(1)} %shard_map.44), channel_id=1, replica_groups=mesh['y'=8,'z'=8,'core'=2,'x'=4] {'y'}, dimensions={0} | all-to-all | bytes 327680 | tf_op jit(solution)/shard_map/all_to_all | solution.py:279
  63.4 0.2 shard_map.45
  63.6 11.8 %all_to_all.55.messages_ref = bf16[8,80,128]{2,1,0:T(8,128)(2,1)S(1)} all-to-all(bf16[8,80,128]{2,1,0:T(8,128)(2,1)S(1)} %shard_map.45), channel_id=1, replica_groups=mesh['y'=8,'z'=8,'core'=2,'x'=4] {'z'}, dimensions={0} | all-to-all | bytes 327680 | tf_op jit(solution)/shard_map/all_to_all | solution.py:281
  75.4 1.1 shard_map.46
  76.5 13.6 %all_to_all.56.panel_ref = bf16[16,32,256]{2,1,0:T(8,128)(2,1)S(1)} all-to-all(bf16[16,32,256]{2,1,0:T(8,128)(2,1)S(1)} %shard_map.46), channel_id=1, replica_groups=mesh['y'=8,'z'=8,'core'=2,'x'=4] {'y','core'}, dimensions={0} | all-to-all | bytes 524288 | tf_op jit(solution)/shard_map/all_to_all | solution.py:289
  90.1 1.4 %shard_map.47 = f32[4,32,512]{2,1,0:T(8,128)S(1)} custom-call(bf16[16,32,256]{2,1,0:T(8,128)(2,1)S(1)} %all_to_all.56.panel_ref, bf16[512,4096]{1,0:T(8,128)(2,1)S(1)} %copy-done), custom_call_target="tpu_custom_call" | custom-call | flops 536870912 | bytes 5242880 | tf_op jit(solution)/shard_map/pallas_call | solution.py:23
  91.5 10.3 %all_to_all.57.parts_ref = f32[4,32,512]{2,1,0:T(8,128)S(1)} all-to-all(f32[4,32,512]{2,1,0:T(8,128)S(1)} %shard_map.47), channel_id=1, replica_groups=mesh['y'=8,'z'=8,'core'=2,'x'=4] {'x'}, dimensions={0} | all-to-all | bytes 524288 | tf_op jit(solution)/shard_map/all_to_all | solution.py:298
  101.8 1.1 shard_map.48
  102.8 4.1 %all_to_all.58.sums_ref = f32[2,520,128]{2,1,0:T(8,128)S(1)} all-to-all(f32[2,520,128]{2,1,0:T(8,128)S(1)} %get-tuple-element.6), channel_id=1, replica_groups=mesh['y'=8,'z'=8,'core'=2,'x'=4] {'core'}, dimensions={0} | all-to-all | bytes 1064960 | tf_op jit(solution)/shard_map/all_to_all | solution.py:308
  106.9 0.1 shard_map.49
  107.0 21.5 %all_to_all.59.messages_ref = bf16[64,24,128]{2,1,0:T(8,128)(2,1)S(1)} all-to-all(bf16[64,24,128]{2,1,0:T(8,128)(2,1)S(1)} %shard_map.49), channel_id=1, replica_groups=mesh['y'=8,'z'=8,'core'=2,'x'=4] {'z','y'}, dimensions={0} | all-to-all | bytes 786432 | tf_op jit(solution)/shard_map/all_to_all | solution.py:310
  128.5 1.8 %shard_map.50 = (f32[32,512]{1,0:T(8,128)}, f32[32,32]{1,0:T(8,128)}) custom-call(bf16[64,24,128]{2,1,0:T(8,128)(2,1)S(1)} %all_to_all.59.messages_ref, f32[32,512]{1,0:T(8,128)S(1)} %get-tuple-element.7.sketch_ref), custom_call_target="tpu_custom_call" | custom-call | flops 1048576 | bytes 1048576 | tf_op jit(solution)/shard_map/pallas_call | solution.py:23
  (1 shorter events, 0.0 us)
Async XLA Ops:
  0.6 0.7 copy-start.1
  1.3 33.4 %copy-start = (bf16[512,4096]{1,0:T(8,128)(2,1)S(1)}, bf16[512,4096]{1,0:T(8,128)(2,1)}, u32[]{:S(2)}) copy-start(bf16[512,4096]{1,0:T(8,128)(2,1)} %transport_ref.7) | copy-start | bytes 12582916

commit v9 on v8

--- a/solution.py
+++ b/solution.py
@@ -9,7 +9,6 @@
 from jax.sharding import Mesh
 from jax.sharding import PartitionSpec as P
 
-CHIPS = ("y", "z")
 RANK = 32
 HIGHEST = lax.Precision.HIGHEST
 F32 = jnp.float32
@@ -94,7 +93,7 @@
 
 
 def first_sketch(tiles_ref, transport_ref, out_ref):
-    cores, chips = tiles_ref.shape[:2]
+    cores, chips = 2, tiles_ref.shape[0] // 2
     cols = transport_ref.shape[1]
     lane = lanes_of((8, 128))
     masks = [(lane >= 32 * q) & (lane < 32 * q + 32) for q in range(4)]
@@ -104,7 +103,8 @@
         rows = []
         for chip in range(start, start + group):
             for core in range(cores):
-                tile = tiles_ref[core, chip].astype(F32)
+                y, z = divmod(chip, 8)
+                tile = tiles_ref[core * chips + z * (chips // 8) + y].astype(F32)
                 rows += [jnp.where(mask, tile, 0.0) for mask in masks]
         at = start * (cols // chips)
         total += jnp.dot(
@@ -154,7 +154,7 @@
     _, gram, columns = product(parts_ref, transport_ref)
     for group in range(groups):
         for core in range(cores):
-            block = columns((group * cores + core) * width, width)
+            block = columns((core * groups + group) * width, width)
             for t in range(width // 32):
                 a, c = t % 4, t // 4
                 at = group * width // 4 + 8 * t
@@ -261,9 +261,8 @@
     flops = 2 * rows * cols * 128
     shape = jax.ShapeDtypeStruct
 
-    copies = kernel_call(fan_out, shape((chips, 8, 128), BF16), 1 << 32, 8 << 20, test_panel)
-    tiles = lax.all_to_all(copies, CHIPS, 0, 0)
-    tiles = lax.all_to_all(jnp.broadcast_to(tiles, (2, chips, 8, 128)), "core", 0, 0)
+    copies = kernel_call(fan_out, shape((2 * chips, 8, 128), BF16), 1 << 32, 8 << 20, test_panel)
+    tiles = lax.all_to_all(copies, ("core", "z", "y"), 0, 0)
     partial = kernel_call(
         first_sketch, shape((nx, RANK, rows), F32), flops, 5 << 20, tiles, transport
     )
@@ -286,7 +285,7 @@
         8 << 20,
         sums,
     )
-    panel = lax.all_to_all(panel, ("y", "core"), 0, 0)
+    panel = lax.all_to_all(panel, ("core", "y"), 0, 0)
     partial = kernel_call(
         next_sketch,
         shape((nx, RANK, rows), F32),

time: 132 us -> 132 us (level)
    all_to_all x2, blocking collectives: 19.8 us -> 18.2 us  [on_device(): parts = lax.all_to_all(partial, 'x', 0, 0)]
    all_to_all x3 -> x2, blocking collectives: 46.9 us -> 47 us  [the longest x1 33.9 us: on_device(): tiles = lax.all_to_all(copies, ('core', 'z', 'y'), 0, 0)]
where the time goes in v9:
time: 132 us; the launch traced here: 130 us
  blocking collectives  121 us (92%)
  Pallas kernels  7.94 us (6%)
    all_to_all x1, blocking collectives, on_device(): tiles = lax.all_to_all(copies, ('core', 'z', 'y'), 0, 0)  33.9 us
    all_to_all x1, blocking collectives, on_device(): sums = lax.all_to_all(sums, ('z', 'y'), 0, 0)  22.7 us
    all_to_all x2, blocking collectives, on_device(): parts = lax.all_to_all(partial, 'x', 0, 0)  18.2 us
    all_to_all x1, blocking collectives, on_device(): panel = lax.all_to_all(panel, ('core', 'y'), 0, 0)  13.1 us
    all_to_all x1, blocking collectives, on_device(): sums = lax.all_to_all(sums, 'y', 0, 0)  12.7 us
    all_to_all x1, blocking collectives, on_device(): sums = lax.all_to_all(sums, 'z', 0, 0)  11.8 us
    all_to_all x2, blocking collectives, on_device(): sums = lax.all_to_all(sums, 'core', 0, 0)  8.26 us
    pallas_call x10, Pallas kernels, kernel_call(): pl.pallas_call(body, out_shape=outs, in_specs=[VMEM] * len(args), out_spe...  7.94 us

profile of v9, /device:TPU:6, one launch (start us, length us, event | category | flops | bytes accessed | tf_op | source)
XLA Modules:
  0.0 130.1 jit_solution(3489449274349437649)
XLA Ops:
  0.6 0.0 copy-start.1
  0.6 0.7 copy-done.1
  1.3 0.0 copy-start
  1.3 0.1 shard_map.41
  1.4 33.9 %all_to_all.45.tiles_ref = bf16[128,8,128]{2,1,0:T(8,128)(2,1)S(1)} all-to-all(bf16[128,8,128]{2,1,0:T(8,128)(2,1)S(1)} %shard_map.41), channel_id=1, replica_groups=mesh['y'=8,'z'=8,'core'=2,'x'=4] {'core','z','y'}, dimensions={0} | all-to-all | bytes 524288 | tf_op jit(solution)/shard_map/all_to_all | solution.py:265
  35.3 0.0 copy-done
  35.3 1.3 %shard_map.42 = f32[4,32,512]{2,1,0:T(8,128)S(1)} custom-call(bf16[128,8,128]{2,1,0:T(8,128)(2,1)S(1)} %all_to_all.45.tiles_ref, bf16[512,4096]{1,0:T(8,128)(2,1)S(1)} %copy-done), custom_call_target="tpu_custom_call" | custom-call | flops 536870912 | bytes 5242880 | tf_op jit(solution)/shard_map/pallas_call | solution.py:22
  36.7 9.2 %all_to_all.46.parts_ref = f32[4,32,512]{2,1,0:T(8,128)S(1)} all-to-all(f32[4,32,512]{2,1,0:T(8,128)S(1)} %shard_map.42), channel_id=1, replica_groups=mesh['y'=8,'z'=8,'core'=2,'x'=4] {'x'}, dimensions={0} | all-to-all | bytes 524288 | tf_op jit(solution)/shard_map/all_to_all | solution.py:269
  45.9 0.9 shard_map.43
  46.8 4.1 %all_to_all.47.sums_ref = f32[2,520,128]{2,1,0:T(8,128)S(1)} all-to-all(f32[2,520,128]{2,1,0:T(8,128)S(1)} %shard_map.43), channel_id=1, replica_groups=mesh['y'=8,'z'=8,'core'=2,'x'=4] {'core'}, dimensions={0} | all-to-all | bytes 1064960 | tf_op jit(solution)/shard_map/all_to_all | solution.py:276
  50.9 0.1 shard_map.44
  51.0 12.7 %all_to_all.48.messages_ref = bf16[8,80,128]{2,1,0:T(8,128)(2,1)S(1)} all-to-all(bf16[8,80,128]{2,1,0:T(8,128)(2,1)S(1)} %shard_map.44), channel_id=1, replica_groups=mesh['y'=8,'z'=8,'core'=2,'x'=4] {'y'}, dimensions={0} | all-to-all | bytes 327680 | tf_op jit(solution)/shard_map/all_to_all | solution.py:278
  63.7 0.2 shard_map.45
  63.9 11.8 %all_to_all.49.messages_ref = bf16[8,80,128]{2,1,0:T(8,128)(2,1)S(1)} all-to-all(bf16[8,80,128]{2,1,0:T(8,128)(2,1)S(1)} %shard_map.45), channel_id=1, replica_groups=mesh['y'=8,'z'=8,'core'=2,'x'=4] {'z'}, dimensions={0} | all-to-all | bytes 327680 | tf_op jit(solution)/shard_map/all_to_all | solution.py:280
  75.7 1.1 shard_map.46
  76.8 13.1 %all_to_all.50.panel_ref = bf16[16,32,256]{2,1,0:T(8,128)(2,1)S(1)} all-to-all(bf16[16,32,256]{2,1,0:T(8,128)(2,1)S(1)} %shard_map.46), channel_id=1, replica_groups=mesh['y'=8,'z'=8,'core'=2,'x'=4] {'core','y'}, dimensions={0} | all-to-all | bytes 524288 | tf_op jit(solution)/shard_map/all_to_all | solution.py:288
  89.8 1.4 %shard_map.47 = f32[4,32,512]{2,1,0:T(8,128)S(1)} custom-call(bf16[16,32,256]{2,1,0:T(8,128)(2,1)S(1)} %all_to_all.50.panel_ref, bf16[512,4096]{1,0:T(8,128)(2,1)S(1)} %copy-done), custom_call_target="tpu_custom_call" | custom-call | flops 536870912 | bytes 5242880 | tf_op jit(solution)/shard_map/pallas_call | solution.py:22
  91.2 9.1 %all_to_all.51.parts_ref = f32[4,32,512]{2,1,0:T(8,128)S(1)} all-to-all(f32[4,32,512]{2,1,0:T(8,128)S(1)} %shard_map.47), channel_id=1, replica_groups=mesh['y'=8,'z'=8,'core'=2,'x'=4] {'x'}, dimensions={0} | all-to-all | bytes 524288 | tf_op jit(solution)/shard_map/all_to_all | solution.py:297
  100.3 1.1 shard_map.48
  101.3 4.1 %all_to_all.52.sums_ref = f32[2,520,128]{2,1,0:T(8,128)S(1)} all-to-all(f32[2,520,128]{2,1,0:T(8,128)S(1)} %get-tuple-element.6), channel_id=1, replica_groups=mesh['y'=8,'z'=8,'core'=2,'x'=4] {'core'}, dimensions={0} | all-to-all | bytes 1064960 | tf_op jit(solution)/shard_map/all_to_all | solution.py:307
  105.4 0.1 shard_map.49
  105.5 22.7 %all_to_all.53.messages_ref = bf16[64,24,128]{2,1,0:T(8,128)(2,1)S(1)} all-to-all(bf16[64,24,128]{2,1,0:T(8,128)(2,1)S(1)} %shard_map.49), channel_id=1, replica_groups=mesh['y'=8,'z'=8,'core'=2,'x'=4] {'z','y'}, dimensions={0} | all-to-all | bytes 786432 | tf_op jit(solution)/shard_map/all_to_all | solution.py:309
  128.3 1.8 %shard_map.50 = (f32[32,512]{1,0:T(8,128)}, f32[32,32]{1,0:T(8,128)}) custom-call(bf16[64,24,128]{2,1,0:T(8,128)(2,1)S(1)} %all_to_all.53.messages_ref, f32[32,512]{1,0:T(8,128)S(1)} %get-tuple-element.7.sketch_ref), custom_call_target="tpu_custom_call" | custom-call | flops 1048576 | bytes 1048576 | tf_op jit(solution)/shard_map/pallas_call | solution.py:22
Async XLA Ops:
  0.6 0.7 copy-start.1
  1.3 34.0 %copy-start = (bf16[512,4096]{1,0:T(8,128)(2,1)S(1)}, bf16[512,4096]{1,0:T(8,128)(2,1)}, u32[]{:S(2)}) copy-start(bf16[512,4096]{1,0:T(8,128)(2,1)} %transport_ref.7) | copy-start | bytes 12582916

commit v10 on v8

--- a/solution.py
+++ b/solution.py
@@ -147,20 +147,15 @@
     return sketch, pack_lower(gram), columns
 
 
-def middle_product(groups, parts_ref, transport_ref, out_ref):
-    cores, height, _ = out_ref.shape
-    cols = transport_ref.shape[1]
-    width = cols // (cores * groups)
+def middle_product(parts_ref, transport_ref, out_ref):
+    groups, height, _ = out_ref.shape
+    width = transport_ref.shape[1] // groups
     _, gram, columns = product(parts_ref, transport_ref)
+    gram = three_terms(gram)
     for group in range(groups):
-        for core in range(cores):
-            block = columns((group * cores + core) * width, width)
-            for t in range(width // 32):
-                a, c = t % 4, t // 4
-                at = group * width // 4 + 8 * t
-                out_ref[core, at : at + 8] = block[8 * a : 8 * a + 8, 128 * c : 128 * c + 128]
-    for core in range(cores):
-        out_ref[core, height - 8 : height] = gram
+        block = columns(group * width, width)
+        tiles = [block[:, 128 * c : 128 * c + 128] for c in range(width // 128)]
+        out_ref[group] = jnp.concatenate(tiles + [gram]).astype(BF16)
 
 
 def last_product(parts_ref, transport_ref, out_ref, sketch_ref):
@@ -272,11 +267,9 @@
     width = cols // (2 * ny)
     height = RANK * width // 128
     sums = kernel_call(
-        functools.partial(middle_product, ny), shape((2, ny * height + 8, 128), F32), flops, 5 << 20, parts, transport
-    )
-    sums = lax.all_to_all(sums, "core", 0, 0)
-    sums = kernel_call(add_cores, shape((ny, height + 16, 128), BF16), 0, 1 << 20, sums)
-    sums = lax.all_to_all(sums, "y", 0, 0)
+        middle_product, shape((2 * ny, height + 16, 128), BF16), flops, 5 << 20, parts, transport
+    )
+    sums = lax.all_to_all(sums, ("core", "y"), 0, 0)
     sums = kernel_call(add_peers, shape((nz, height + 16, 128), BF16), 0, 1 << 20, sums)
     sums = lax.all_to_all(sums, "z", 0, 0)
     panel = kernel_call(
@@ -286,7 +279,7 @@
         8 << 20,
         sums,
     )
-    panel = lax.all_to_all(panel, ("y", "core"), 0, 0)
+    panel = lax.all_to_all(panel, ("core", "y"), 0, 0)
     partial = kernel_call(
         next_sketch,
         shape((nx, RANK, rows), F32),

time: 132 us -> 131 us (level)
    all_to_all x2 -> x1, blocking collectives: 8.26 us -> 4.13 us  [on_device(): sums = lax.all_to_all(sums, 'core', 0, 0)]
    all_to_all x2, blocking collectives: 26.4 us -> 29.5 us  [the longest x1 15.1 us: on_device(): panel = lax.all_to_all(panel, ('core', 'y'), 0, 0)]
    all_to_all x1, blocking collectives: 21.5 us -> 22.8 us  [on_device(): sums = lax.all_to_all(sums, ('z', 'y'), 0, 0)]
    pallas_call x10 -> x9, Pallas kernels: 7.93 us -> 7.86 us  [kernel_call(): pl.pallas_call(body, out_shape=outs, in_specs=[VMEM] * len(args), out_spe...]
where the time goes in v10:
time: 131 us; the launch traced here: 129 us
  blocking collectives  120 us (92%)
  Pallas kernels  7.86 us (6%)
    all_to_all x1, blocking collectives, on_device(): tiles = lax.all_to_all(copies, CHIPS, 0, 0)  29.4 us
    all_to_all x1, blocking collectives, on_device(): sums = lax.all_to_all(sums, ('z', 'y'), 0, 0)  22.8 us
    all_to_all x2, blocking collectives, on_device(): parts = lax.all_to_all(partial, 'x', 0, 0)  18.5 us
    all_to_all x1, blocking collectives, on_device(): panel = lax.all_to_all(panel, ('core', 'y'), 0, 0)  15.1 us
    all_to_all x1, blocking collectives, on_device(): sums = lax.all_to_all(sums, ('core', 'y'), 0, 0)  14.4 us
    all_to_all x1, blocking collectives, on_device(): sums = lax.all_to_all(sums, 'z', 0, 0)  11.9 us
    pallas_call x9, Pallas kernels, kernel_call(): pl.pallas_call(body, out_shape=outs, in_specs=[VMEM] * len(args), out_spe...  7.86 us
    all_to_all x1, blocking collectives, on_device(): sums = lax.all_to_all(sums, 'core', 0, 0)  4.13 us

profile of v10, /device:TPU:6, one launch (start us, length us, event | category | flops | bytes accessed | tf_op | source)
XLA Modules:
  0.0 129.5 jit_solution(2657310092388456304)
XLA Ops:
  0.6 0.0 copy-start.1
  0.6 0.7 copy-done.1
  1.3 0.0 copy-start
  1.3 0.1 shard_map.41
  1.4 29.4 %all_to_all.45 = bf16[64,8,128]{2,1,0:T(8,128)(2,1)S(1)} all-to-all(bf16[64,8,128]{2,1,0:T(8,128)(2,1)S(1)} %shard_map.41), channel_id=1, replica_groups=mesh['y'=8,'z'=8,'core'=2,'x'=4] {'y','z'}, dimensions={0} | all-to-all | bytes 262144 | tf_op jit(solution)/shard_map/all_to_all | solution.py:260
  30.8 3.9 %all_to_all.46.tiles_ref = bf16[2,64,8,128]{3,2,1,0:T(8,128)(2,1)S(1)} all-to-all(bf16[2,64,8,128]{3,2,1,0:T(8,128)(2,1)S(1)} %broadcast_in_dim.3), channel_id=1, replica_groups=mesh['y'=8,'z'=8,'core'=2,'x'=4] {'core'}, dimensions={0} | all-to-all | bytes 524288 | tf_op jit(solution)/shard_map/all_to_all | solution.py:261
  34.7 0.0 copy-done
  34.7 1.3 %shard_map.42 = f32[4,32,512]{2,1,0:T(8,128)S(1)} custom-call(bf16[2,64,8,128]{3,2,1,0:T(8,128)(2,1)S(1)} %all_to_all.46.tiles_ref, bf16[512,4096]{1,0:T(8,128)(2,1)S(1)} %copy-done), custom_call_target="tpu_custom_call" | custom-call | flops 536870912 | bytes 5242880 | tf_op jit(solution)/shard_map/pallas_call | solution.py:23
  36.1 9.5 %all_to_all.47.parts_ref = f32[4,32,512]{2,1,0:T(8,128)S(1)} all-to-all(f32[4,32,512]{2,1,0:T(8,128)S(1)} %shard_map.42), channel_id=1, replica_groups=mesh['y'=8,'z'=8,'core'=2,'x'=4] {'x'}, dimensions={0} | all-to-all | bytes 524288 | tf_op jit(solution)/shard_map/all_to_all | solution.py:265
  45.6 0.9 shard_map.43
  46.5 14.4 %all_to_all.48.messages_ref = bf16[16,80,128]{2,1,0:T(8,128)(2,1)S(1)} all-to-all(bf16[16,80,128]{2,1,0:T(8,128)(2,1)S(1)} %shard_map.43), channel_id=1, replica_groups=mesh['y'=8,'z'=8,'core'=2,'x'=4] {'core','y'}, dimensions={0} | all-to-all | bytes 655360 | tf_op jit(solution)/shard_map/all_to_all | solution.py:272
  60.9 0.2 shard_map.44
  61.0 11.9 %all_to_all.49.messages_ref = bf16[8,80,128]{2,1,0:T(8,128)(2,1)S(1)} all-to-all(bf16[8,80,128]{2,1,0:T(8,128)(2,1)S(1)} %shard_map.44), channel_id=1, replica_groups=mesh['y'=8,'z'=8,'core'=2,'x'=4] {'z'}, dimensions={0} | all-to-all | bytes 327680 | tf_op jit(solution)/shard_map/all_to_all | solution.py:274
  72.9 1.1 shard_map.45
  74.0 15.1 %all_to_all.50.panel_ref = bf16[16,32,256]{2,1,0:T(8,128)(2,1)S(1)} all-to-all(bf16[16,32,256]{2,1,0:T(8,128)(2,1)S(1)} %shard_map.45), channel_id=1, replica_groups=mesh['y'=8,'z'=8,'core'=2,'x'=4] {'core','y'}, dimensions={0} | all-to-all | bytes 524288 | tf_op jit(solution)/shard_map/all_to_all | solution.py:282
  89.1 1.4 %shard_map.46 = f32[4,32,512]{2,1,0:T(8,128)S(1)} custom-call(bf16[16,32,256]{2,1,0:T(8,128)(2,1)S(1)} %all_to_all.50.panel_ref, bf16[512,4096]{1,0:T(8,128)(2,1)S(1)} %copy-done), custom_call_target="tpu_custom_call" | custom-call | flops 536870912 | bytes 5242880 | tf_op jit(solution)/shard_map/pallas_call | solution.py:23
  90.5 9.1 %all_to_all.51.parts_ref = f32[4,32,512]{2,1,0:T(8,128)S(1)} all-to-all(f32[4,32,512]{2,1,0:T(8,128)S(1)} %shard_map.46), channel_id=1, replica_groups=mesh['y'=8,'z'=8,'core'=2,'x'=4] {'x'}, dimensions={0} | all-to-all | bytes 524288 | tf_op jit(solution)/shard_map/all_to_all | solution.py:291
  99.6 1.1 shard_map.47
  100.6 4.1 %all_to_all.52.sums_ref = f32[2,520,128]{2,1,0:T(8,128)S(1)} all-to-all(f32[2,520,128]{2,1,0:T(8,128)S(1)} %get-tuple-element.6), channel_id=1, replica_groups=mesh['y'=8,'z'=8,'core'=2,'x'=4] {'core'}, dimensions={0} | all-to-all | bytes 1064960 | tf_op jit(solution)/shard_map/all_to_all | solution.py:301
  104.7 0.1 shard_map.48
  104.8 22.8 %all_to_all.53.messages_ref = bf16[64,24,128]{2,1,0:T(8,128)(2,1)S(1)} all-to-all(bf16[64,24,128]{2,1,0:T(8,128)(2,1)S(1)} %shard_map.48), channel_id=1, replica_groups=mesh['y'=8,'z'=8,'core'=2,'x'=4] {'z','y'}, dimensions={0} | all-to-all | bytes 786432 | tf_op jit(solution)/shard_map/all_to_all | solution.py:303
  127.7 1.8 %shard_map.49 = (f32[32,512]{1,0:T(8,128)}, f32[32,32]{1,0:T(8,128)}) custom-call(bf16[64,24,128]{2,1,0:T(8,128)(2,1)S(1)} %all_to_all.53.messages_ref, f32[32,512]{1,0:T(8,128)S(1)} %get-tuple-element.7.sketch_ref), custom_call_target="tpu_custom_call" | custom-call | flops 1048576 | bytes 1048576 | tf_op jit(solution)/shard_map/pallas_call | solution.py:23
  (1 shorter events, 0.0 us)
Async XLA Ops:
  0.6 0.7 copy-start.1
  1.3 33.4 %copy-start = (bf16[512,4096]{1,0:T(8,128)(2,1)S(1)}, bf16[512,4096]{1,0:T(8,128)(2,1)}, u32[]{:S(2)}) copy-start(bf16[512,4096]{1,0:T(8,128)(2,1)} %transport_ref.7) | copy-start | bytes 12582916

commit v11 on v10

--- a/solution.py
+++ b/solution.py
@@ -159,8 +159,7 @@
 
 
 def last_product(parts_ref, transport_ref, out_ref, sketch_ref):
-    cores, height, _ = out_ref.shape
-    chips = height // 8 - 1
+    chips = out_ref.shape[0] * 4
     sketch, gram, columns = product(parts_ref, transport_ref)
     sketch_ref[...] = sketch
     lane = lanes_of((8, 128))
@@ -179,10 +178,10 @@
                 for b, v in ((a, v0), (a + 1, v1)):
                     device = 16 * wide + 4 * c + b
                     y, z = divmod(device // 2, 8)
-                    at = 8 * (z * (chips // 8) + y)
-                    out_ref[device % 2, at : at + 8] = v
-    for core in range(cores):
-        out_ref[core, height - 8 : height] = gram
+                    out_ref[device % 2 * 8 + y, 8 * z : 8 * z + 8] = v.astype(BF16)
+    gram = three_terms(gram).astype(BF16)
+    for group in range(out_ref.shape[0]):
+        out_ref[group, 64:80] = gram
 
 
 def three_terms(gram):
@@ -208,14 +207,13 @@
     return jnp.concatenate([total[:-16], jnp.where(lane < 80, gram, 0.0)])
 
 
-def add_cores(sums_ref, out_ref):
-    peers, height, _ = out_ref.shape
-    rows = height - 16
-    gram = three_terms(sums_ref[0, peers * rows :] + sums_ref[1, peers * rows :])
-    for peer in range(peers):
-        at = slice(peer * rows, (peer + 1) * rows)
-        block = sums_ref[0, at] + sums_ref[1, at]
-        out_ref[peer] = jnp.concatenate([block, gram]).astype(BF16)
+def split_tiles(messages_ref, out_ref):
+    total = decoded_sum(messages_ref)
+    gram = three_terms(total[-8:])
+    for z in range(out_ref.shape[0]):
+        tile = total[8 * z : 8 * z + 8]
+        high = tile.astype(BF16).astype(F32)
+        out_ref[z] = jnp.concatenate([high, tile - high, gram]).astype(BF16)
 
 
 def add_peers(messages_ref, out_ref):
@@ -238,11 +236,11 @@
 
 def finish(total_rows, messages_ref, sketch_ref, basis_ref, coimage_ref):
     total = decoded_sum(messages_ref)
-    inverse = inverse_factor(unpack_lower(total[8:]) / total_rows)
+    inverse = inverse_factor(unpack_lower(total[16:]) / total_rows)
     basis_ref[...] = jnp.dot(
         inverse, sketch_ref[...], precision=HIGHEST, preferred_element_type=F32
     )
-    block = unpack_square(total[0:8])[:, :RANK]
+    block = unpack_square(total[0:8] + total[8:16])[:, :RANK]
     coimage_ref[...] = lax.dot_general(
         block, inverse, (((0,), (1,)), ((), ())), precision=HIGHEST, preferred_element_type=F32
     )
@@ -292,15 +290,15 @@
 
     sums, sketch = kernel_call(
         last_product,
-        (shape((2, 8 * chips + 8, 128), F32), shape((RANK, rows), F32)),
+        (shape((2 * ny, 8 * nz + 16, 128), BF16), shape((RANK, rows), F32)),
         flops,
         6 << 20,
         parts,
         transport,
     )
-    sums = lax.all_to_all(sums, "core", 0, 0)
-    sums = kernel_call(add_cores, shape((chips, 24, 128), BF16), 0, 1 << 20, sums)
-    sums = lax.all_to_all(sums, ("z", "y"), 0, 0)
+    sums = lax.all_to_all(sums, ("core", "y"), 0, 0)
+    sums = kernel_call(split_tiles, shape((nz, 32, 128), BF16), 0, 1 << 20, sums)
+    sums = lax.all_to_all(sums, "z", 0, 0)
     basis, coimage = kernel_call(
         functools.partial(finish, total_rows),
         (shape((RANK, rows), F32), shape((RANK, RANK), F32)),

time: 131 us -> 132 us (level)
  the two profiles are of different devices: /device:TPU:6 before, /device:TPU:8 now
where the time goes in v11:
time: 132 us
  blocking collectives  123 us (93%)
  Pallas kernels  7.85 us (6%)
    all_to_all x2, blocking collectives, on_device(): sums = lax.all_to_all(sums, ('core', 'y'), 0, 0)  32.5 us
    all_to_all x1, blocking collectives, on_device(): tiles = lax.all_to_all(copies, CHIPS, 0, 0)  28.3 us
    all_to_all x2, blocking collectives, on_device(): sums = lax.all_to_all(sums, 'z', 0, 0)  22.5 us
    all_to_all x2, blocking collectives, on_device(): parts = lax.all_to_all(partial, 'x', 0, 0)  20.1 us
    all_to_all x1, blocking collectives, on_device(): panel = lax.all_to_all(panel, ('core', 'y'), 0, 0)  15.2 us
    pallas_call x9, Pallas kernels, kernel_call(): pl.pallas_call(body, out_shape=outs, in_specs=[VMEM] * len(args), out_spe...  7.85 us
    all_to_all x1, blocking collectives, on_device(): lax.all_to_all(jnp.broadcast_to(tiles, (2, chips, 8, 128)), 'core', 0, 0)  3.94 us

profile of v11, /device:TPU:8, one launch (start us, length us, event | category | flops | bytes accessed | tf_op | source)
XLA Modules:
  0.0 131.8 jit_solution(13111425900100289320)
XLA Ops:
  0.6 0.0 copy-start.1
  0.6 0.7 copy-done.1
  1.3 0.0 copy-start
  1.3 0.1 shard_map.41
  1.4 28.3 %all_to_all.45 = bf16[64,8,128]{2,1,0:T(8,128)(2,1)S(1)} all-to-all(bf16[64,8,128]{2,1,0:T(8,128)(2,1)S(1)} %shard_map.41), channel_id=1, replica_groups=mesh['y'=8,'z'=8,'core'=2,'x'=4] {'y','z'}, dimensions={0} | all-to-all | bytes 262144 | tf_op jit(solution)/shard_map/all_to_all | solution.py:258
  29.7 3.9 %all_to_all.46.tiles_ref = bf16[2,64,8,128]{3,2,1,0:T(8,128)(2,1)S(1)} all-to-all(bf16[2,64,8,128]{3,2,1,0:T(8,128)(2,1)S(1)} %broadcast_in_dim.3), channel_id=1, replica_groups=mesh['y'=8,'z'=8,'core'=2,'x'=4] {'core'}, dimensions={0} | all-to-all | bytes 524288 | tf_op jit(solution)/shard_map/all_to_all | solution.py:259
  33.7 0.0 copy-done
  33.7 1.3 shard_map.42
  35.0 11.1 %all_to_all.47.parts_ref = f32[4,32,512]{2,1,0:T(8,128)S(1)} all-to-all(f32[4,32,512]{2,1,0:T(8,128)S(1)} %shard_map.42), channel_id=1, replica_groups=mesh['y'=8,'z'=8,'core'=2,'x'=4] {'x'}, dimensions={0} | all-to-all | bytes 524288 | tf_op jit(solution)/shard_map/all_to_all | solution.py:263
  46.1 0.9 shard_map.43
  47.0 16.3 %all_to_all.48.messages_ref = bf16[16,80,128]{2,1,0:T(8,128)(2,1)S(1)} all-to-all(bf16[16,80,128]{2,1,0:T(8,128)(2,1)S(1)} %shard_map.43), channel_id=1, replica_groups=mesh['y'=8,'z'=8,'core'=2,'x'=4] {'core','y'}, dimensions={0} | all-to-all | bytes 655360 | tf_op jit(solution)/shard_map/all_to_all | solution.py:270
  63.3 0.2 shard_map.44
  63.4 11.8 %all_to_all.49.messages_ref = bf16[8,80,128]{2,1,0:T(8,128)(2,1)S(1)} all-to-all(bf16[8,80,128]{2,1,0:T(8,128)(2,1)S(1)} %shard_map.44), channel_id=1, replica_groups=mesh['y'=8,'z'=8,'core'=2,'x'=4] {'z'}, dimensions={0} | all-to-all | bytes 327680 | tf_op jit(solution)/shard_map/all_to_all | solution.py:272
  75.2 1.1 shard_map.45
  76.3 15.2 %all_to_all.50.panel_ref = bf16[16,32,256]{2,1,0:T(8,128)(2,1)S(1)} all-to-all(bf16[16,32,256]{2,1,0:T(8,128)(2,1)S(1)} %shard_map.45), channel_id=1, replica_groups=mesh['y'=8,'z'=8,'core'=2,'x'=4] {'core','y'}, dimensions={0} | all-to-all | bytes 524288 | tf_op jit(solution)/shard_map/all_to_all | solution.py:280
  91.6 1.4 %shard_map.46 = f32[4,32,512]{2,1,0:T(8,128)S(1)} custom-call(bf16[16,32,256]{2,1,0:T(8,128)(2,1)S(1)} %all_to_all.50.panel_ref, bf16[512,4096]{1,0:T(8,128)(2,1)S(1)} %copy-done), custom_call_target="tpu_custom_call" | custom-call | flops 536870912 | bytes 5242880 | tf_op jit(solution)/shard_map/pallas_call | solution.py:23
  92.9 9.1 %all_to_all.51.parts_ref = f32[4,32,512]{2,1,0:T(8,128)S(1)} all-to-all(f32[4,32,512]{2,1,0:T(8,128)S(1)} %shard_map.46), channel_id=1, replica_groups=mesh['y'=8,'z'=8,'core'=2,'x'=4] {'x'}, dimensions={0} | all-to-all | bytes 524288 | tf_op jit(solution)/shard_map/all_to_all | solution.py:289
  102.0 1.1 shard_map.47
  103.1 16.2 %all_to_all.52.messages_ref = bf16[16,80,128]{2,1,0:T(8,128)(2,1)S(1)} all-to-all(bf16[16,80,128]{2,1,0:T(8,128)(2,1)S(1)} %get-tuple-element.6), channel_id=1, replica_groups=mesh['y'=8,'z'=8,'core'=2,'x'=4] {'core','y'}, dimensions={0} | all-to-all | bytes 655360 | tf_op jit(solution)/shard_map/all_to_all | solution.py:299
  119.2 0.2 shard_map.48
  119.4 10.7 %all_to_all.53.messages_ref = bf16[8,32,128]{2,1,0:T(8,128)(2,1)S(1)} all-to-all(bf16[8,32,128]{2,1,0:T(8,128)(2,1)S(1)} %shard_map.48), channel_id=1, replica_groups=mesh['y'=8,'z'=8,'core'=2,'x'=4] {'z'}, dimensions={0} | all-to-all | bytes 131072 | tf_op jit(solution)/shard_map/all_to_all | solution.py:301
  130.1 1.7 %shard_map.49 = (f32[32,512]{1,0:T(8,128)}, f32[32,32]{1,0:T(8,128)}) custom-call(bf16[8,32,128]{2,1,0:T(8,128)(2,1)S(1)} %all_to_all.53.messages_ref, f32[32,512]{1,0:T(8,128)S(1)} %get-tuple-element.7.sketch_ref), custom_call_target="tpu_custom_call" | custom-call | flops 1048576 | bytes 1048576 | tf_op jit(solution)/shard_map/pallas_call | solution.py:23
  (1 shorter events, 0.0 us)
Async XLA Ops:
  0.6 0.7 copy-start.1
  1.3 32.3 %copy-start = (bf16[512,4096]{1,0:T(8,128)(2,1)S(1)}, bf16[512,4096]{1,0:T(8,128)(2,1)}, u32[]{:S(2)}) copy-start(bf16[512,4096]{1,0:T(8,128)(2,1)} %transport_ref.7) | copy-start | bytes 12582916
